TPU v7x, 256 devices: a whole 4x4x8 slice. The times are simulated.
256 devices in a mesh: seq: 4 (over x), ctx: 64 (over z, y, core).
Axes of the slice: x: 4, y: 4, z: 8, core: 2. Of those that a mesh axis runs over, the one named last changes fastest.
Arguments:
- queries: bfloat16 [32768, 2048], P(('seq', 'ctx')), parts along dimension 0, may hold values from -1 to 1
- keys_in: bfloat16 [32768, 2048], P(('seq', 'ctx')), parts along dimension 0, may hold values from -1 to 1
- value_input: bfloat16 [32768, 2048], P(('seq', 'ctx')), parts along dimension 0, may hold values from -1 to 1
- level_gain: float32 [14, 16, 32768], P(None, None, ('seq', 'ctx')), parts along dimension 2, may hold values from 0.2 to 2
- decay_log: float32 [16, 32768], P(None, ('seq', 'ctx')), parts along dimension 1, may hold values from -0.7 to 0, as said below
- out_grad: bfloat16 [32768, 2048], P(('seq', 'ctx')), parts along dimension 0, may hold values from -1 to 1
Outputs:
- mixed_out: bfloat16 [32768, 2048], P(('seq', 'ctx')), parts along dimension 0
- query_gradient: bfloat16 [32768, 2048], P(('seq', 'ctx')), parts along dimension 0
- grad_keys: bfloat16 [32768, 2048], P(('seq', 'ctx')), parts along dimension 0
- grad_values: bfloat16 [32768, 2048], P(('seq', 'ctx')), parts along dimension 0
- grad_gain: float32 [14, 16, 32768], P(None, None, ('seq', 'ctx')), parts along dimension 2
- grad_decay: float32 [16, 32768], P(None, ('seq', 'ctx')), parts along dimension 1
There are 4 independent parts, one for each index of `seq`. A program takes and returns all parts, laid end to end along the dimension named above; each array names one. Nothing has to cross between parts.
Inputs may be any that keep to these rules, and one draw needn't show every extreme that they name: `decay_log`: every entry is negative.
All inputs are finite; a program needn't handle non-finite values.
Results may differ from a plain program's by a relative error of at most 0.001.
Values sent between devices are 32-bit elements; how exact they have to be, the bound alone decides.
A program may use at most 128 MiB of HBM per device.

v0:
```python
import jax
import jax.numpy as jnp
from jax import lax
from jax.sharding import PartitionSpec as P

TOP_ACCURACY = lax.Precision.HIGHEST


def from_partner(block, axis, distance):
    count = lax.axis_size(axis)
    route = []
    for low in range(count):
        high = low | 1 << distance
        if high != low and high < count:
            route += [(low, high), (high, low)]
    return lax.ppermute(block, axis, route)


def passed_along(value, axis, steps):
    count = lax.axis_size(axis)
    first, last = (max(0, -steps), min(count, count - steps))
    return lax.ppermute(value, axis, [(source, source + steps) for source in range(first, last)])


def level_table(tok, lvl_in):
    places = jnp.arange(tok, dtype=jnp.int32)
    mixing = jnp.bitwise_xor(places[:, None], places[None, :])
    table = jnp.zeros((tok, tok), jnp.int32)
    for power in range(lvl_in):
        table = table + (mixing >= 2**power).astype(jnp.int32)
    return table


def block_front(keys_h, value_rows_head, decay):
    running = jnp.cumsum(decay, axis=1)
    total_sum = running[:, -1]
    scaled_result = keys_h * jnp.exp(total_sum[:, None] - running)[:, :, None]
    return (
        jnp.einsum("ybu,ybe->yue", scaled_result, value_rows_head, precision=TOP_ACCURACY),
        total_sum,
    )


def block_output(queries_h, keys_h, value_rows_head, gain, decay, buckets):
    tok = queries_h.shape[1]
    lvl_in = tok.bit_length() - 1
    running = jnp.cumsum(decay, axis=1)
    places = jnp.arange(tok, dtype=jnp.int32)
    causal = places[:, None] >= places[None, :]
    spread_gap = jnp.where(causal[None], running[:, :, None] - running[:, None, :], 0.0)
    fading = jnp.where(causal[None], jnp.exp(spread_gap), 0.0)
    table = level_table(tok, lvl_in)
    picks = (table[None] == jnp.arange(lvl_in + 1, dtype=jnp.int32)[:, None, None]).astype(
        jnp.float32
    )
    weighting = jnp.einsum("lij,lhi->hij", picks, gain[: lvl_in + 1], precision=TOP_ACCURACY)
    scores = jnp.einsum("hik,hjk->hij", queries_h, keys_h, precision=TOP_ACCURACY)
    result = jnp.einsum(
        "hij,hjv->hiv", scores * weighting * fading, value_rows_head, precision=TOP_ACCURACY
    )
    lifted = queries_h * jnp.exp(running)[:, :, None]
    reach = gain[lvl_in + 1 :][:, :, :, None] * lifted[None]
    return result + jnp.einsum("jhik,jhkv->hiv", reach, buckets, precision=TOP_ACCURACY)


def merge_step(own_total, own_state, offset, other_total, other_state, is_upper):
    bucket = jnp.where(is_upper, jnp.exp(offset)[:, None, None] * other_state, 0.0)
    low_state = jnp.where(is_upper, other_state, own_state)
    high_state = jnp.where(is_upper, own_state, other_state)
    high_total = jnp.where(is_upper, own_total, other_total)
    merged = jnp.exp(high_total)[:, None, None] * low_state + high_state
    new_offset = offset + jnp.where(is_upper, other_total, 0.0)
    return (own_total + other_total, merged, new_offset, bucket)


def partner_grads(
    own_total, own_state, offset, other_total, g_total, g_state, g_offset, g_bucket, is_upper
):
    factor = jnp.exp(jnp.where(is_upper, own_total, other_total))
    d_other_state = jnp.where(
        is_upper,
        factor[:, None, None] * g_state + jnp.exp(offset)[:, None, None] * g_bucket,
        g_state,
    )
    lower_term = factor * jnp.sum(g_state * own_state, axis=(1, 2))
    d_other_total = g_total + jnp.where(is_upper, g_offset, lower_term)
    return (d_other_total, d_other_state)


def own_grads(
    own_total, offset, other_total, other_state, g_total, g_state, g_offset, g_bucket, is_upper
):
    factor = jnp.exp(jnp.where(is_upper, own_total, other_total))
    d_own_state = jnp.where(is_upper, g_state, factor[:, None, None] * g_state)
    upper_total = factor * jnp.sum(g_state * other_state, axis=(1, 2))
    d_own_total = g_total + jnp.where(is_upper, upper_total, 0.0)
    upper_offset = jnp.exp(offset) * jnp.sum(g_bucket * other_state, axis=(1, 2))
    d_offset = g_offset + jnp.where(is_upper, upper_offset, 0.0)
    return (d_own_total, d_own_state, d_offset)


def to_heads(block, heads):
    tokens, width = block.shape
    return block.reshape(tokens, heads, width // heads).transpose(1, 0, 2).astype(jnp.float32)


def from_heads(block):
    heads, tokens, head_dim = block.shape
    return block.transpose(1, 0, 2).reshape(tokens, heads * head_dim)


def per_device(queries, keys_in, value_input, level_gain, decay_log, out_grad):
    heads = decay_log.shape[0]
    query_h = to_heads(queries, heads)
    key_h = to_heads(keys_in, heads)
    value_h = to_heads(value_input, heads)
    cotangent = to_heads(out_grad, heads)
    count = lax.axis_size("ctx")
    depth = count.bit_length() - 1
    position = lax.axis_index("ctx")
    (state, total_sum), front_back = jax.vjp(block_front, key_h, value_h, decay_log)
    own_total = total_sum
    own_state = state
    offset = jnp.zeros_like(total_sum)
    saved = []
    found = []
    top_other = state
    for bit in range(depth):
        other_total, other_state = from_partner((own_total, own_state), "ctx", bit)
        is_upper = jnp.right_shift(position, bit) % 2 == 1
        saved.append((own_total, own_state, offset, other_total))
        if bit == depth - 1:
            top_other = other_state
        own_total, own_state, offset, bucket = merge_step(
            own_total, own_state, offset, other_total, other_state, is_upper
        )
        found.append(bucket)
    buckets = jnp.stack(found)
    mixed, out_back = jax.vjp(block_output, query_h, key_h, value_h, level_gain, decay_log, buckets)
    grad_query, grad_key, grad_value, grad_gain, grad_decay, bucket_gradient = out_back(cotangent)
    grad_total = jnp.zeros_like(total_sum)
    grad_state = jnp.zeros_like(state)
    grad_offset = jnp.zeros_like(total_sum)
    for bit in reversed(range(depth)):
        is_upper = jnp.right_shift(position, bit) % 2 == 1
        level_total, level_state, level_offset, level_other_total = saved[bit]
        d_other_total, d_other_state = partner_grads(
            level_total,
            level_state,
            level_offset,
            level_other_total,
            grad_total,
            grad_state,
            grad_offset,
            bucket_gradient[bit],
            is_upper,
        )
        if bit == depth - 1:
            back_total, back_state = passed_along(
                (d_other_total, d_other_state), "ctx", -(count // 2)
            )
            partner_state = top_other
        else:
            back_total, back_state, partner_state = from_partner(
                (d_other_total, d_other_state, level_state), "ctx", bit
            )
        d_own_total, d_own_state, d_offset = own_grads(
            level_total,
            level_offset,
            level_other_total,
            partner_state,
            grad_total,
            grad_state,
            grad_offset,
            bucket_gradient[bit],
            is_upper,
        )
        grad_total = d_own_total + back_total
        grad_state = d_own_state + back_state
        grad_offset = d_offset
    key_more, value_more, decay_more = front_back((grad_state, grad_total))
    return (
        from_heads(mixed).astype(jnp.bfloat16),
        from_heads(grad_query).astype(jnp.bfloat16),
        from_heads(grad_key + key_more).astype(jnp.bfloat16),
        from_heads(grad_value + value_more).astype(jnp.bfloat16),
        grad_gain,
        grad_decay + decay_more,
    )


def solution(mesh):
    placed = (
        P(("seq", "ctx"), None),
        P(("seq", "ctx"), None),
        P(("seq", "ctx"), None),
        P(None, None, ("seq", "ctx")),
        P(None, ("seq", "ctx")),
        P(("seq", "ctx"), None),
    )
    return jax.shard_map(
        per_device,
        mesh=mesh,
        in_specs=placed,
        out_specs=(
            P(("seq", "ctx"), None),
            P(("seq", "ctx"), None),
            P(("seq", "ctx"), None),
            P(("seq", "ctx"), None),
            P(None, None, ("seq", "ctx")),
            P(None, ("seq", "ctx")),
        ),
        check_vma=False,
    )
```

profile of v0, /device:TPU:1, one launch (start us, length us, event | category | flops | bytes accessed | tf_op | source)
XLA Modules:
  0.0 421.4 jit_solution(8103557414962444258)
XLA Ops:
  1.9 1.3 copy.65
  3.2 1.7 fusion.28
  4.9 3.3 collective-permute-start
  8.3 2.2 collective-permute-done.1
  10.5 1.3 select_add_fusion.4
  11.9 1.5 collective-permute-start.3
  13.3 23.2 %collective-permute-done.3 = f32[16]{0:T(128)S(1)} collective-permute-done((f32[16]{0:T(128)S(1)}, f32[16]{0:T(128)S(1)}, u32[]{:S(2)}, u32[]{:S(2)}) %collective-permute-start.3) | collective-permute-done | bytes 96 | tf_op jit(solution)/shard_map/ppermute | solution.py:16
  36.6 2.7 select_add_fusion.3
  40.5 1.8 collective-permute-start.5
  42.3 22.4 %collective-permute-done.5 = f32[16]{0:T(128)S(1)} collective-permute-done((f32[16]{0:T(128)S(1)}, f32[16]{0:T(128)S(1)}, u32[]{:S(2)}, u32[]{:S(2)}) %collective-permute-start.5) | collective-permute-done | bytes 96 | tf_op jit(solution)/shard_map/ppermute | solution.py:16
  64.6 2.8 select_add_fusion.2
  67.4 1.5 collective-permute-start.7
  68.9 21.5 %collective-permute-done.7 = f32[16]{0:T(128)S(1)} collective-permute-done((f32[16]{0:T(128)S(1)}, f32[16]{0:T(128)S(1)}, u32[]{:S(2)}, u32[]{:S(2)}) %collective-permute-start.7) | collective-permute-done | bytes 96 | tf_op jit(solution)/shard_map/ppermute | solution.py:16
  90.4 2.8 select_add_fusion.1
  93.2 1.6 collective-permute-start.8
  94.9 1.3 copy.64
  98.0 1.3 copy.107
  99.4 42.4 %collective-permute-done.9 = f32[16]{0:T(128)S(1)} collective-permute-done((f32[16]{0:T(128)S(1)}, f32[16]{0:T(128)S(1)}, u32[]{:S(2)}, u32[]{:S(2)}) %collective-permute-start.9) | collective-permute-done | bytes 96 | tf_op jit(solution)/shard_map/ppermute | solution.py:16
  141.8 5.1 %collective-permute-start.11 = (f32[16]{0:T(128)S(1)}, f32[16]{0:T(128)S(1)}, u32[]{:S(2)}, u32[]{:S(2)}) collective-permute-start(f32[16]{0:T(128)S(1)} %get-tuple-element.79), channel_id=1, source_target_pairs={{0,32},{32,0},{1,33},{33,1},{2,34},{34,2},{3,35},{35,3},{4,36},{36... | collective-permute-start | bytes 200 | tf_op jit(solution)/shard_map/ppermute | solution.py:16
  147.0 1.4 bitcast_dynamic-update-slice_fusion.4
  148.4 2.0 multiply_reduce_fusion.15
  150.9 1.4 bitcast_dynamic-update-slice_fusion.3
  152.3 1.4 bitcast_dynamic-update-slice_fusion.2
  153.7 1.4 bitcast_dynamic-update-slice_fusion.1
  155.1 43.0 %collective-permute-done.10 = f32[16,128,128]{2,1,0:T(8,128)S(1)} collective-permute-done((f32[16,128,128]{2,1,0:T(8,128)S(1)}, f32[16,128,128]{2,1,0:T(8,128)S(1)}, u32[]{:S(2)}, u32[]{:S(2)}) %collective-permute-start.10) | collective-permute-done | bytes 1048608 | tf_op jit(solution)/shard_map/ppermute | solution.py:16
  199.1 5.5 %fusion.1 = (f32[6,16,128]{2,0,1:T(8,128)S(1)}, f32[16,128,128]{1,2,0:T(8,128)}, f32[6,16,128,128]{2,3,0,1:T(8,128)S(1)}) fusion(f32[16,128,128]{1,2,0:T(8,128)S(1)} %copy-done.9, f32[6,16,128]{2,0,1:T(8,128)S(1)} %copy.72, bf16[16,128,128,1]{1,2,3,0:T(8,128)(2,1)S(1)} %bitcast.179, f32[6,16,128,128]{3,2,1,0:T(8,128)S(1)} %bitcast_dynamic-update-slice_fusion), kind=kOutput, calls=%fused_computation.3 | convolution fusion | flops 2423508992 | bytes 15302656 | tf_op jit(solution)/shard_map/transpose(jvp(jhik,jhkv->hiv))/dot_general | solution.py:63
  204.6 3.0 fusion.8
  207.9 1.3 collective-permute-start.12
  209.2 27.2 %collective-permute-done.12 = f32[16,128,128]{2,1,0:T(8,128)S(1)} collective-permute-done((f32[16,128,128]{2,1,0:T(8,128)S(1)}, f32[16,128,128]{2,1,0:T(8,128)S(1)}, u32[]{:S(2)}, u32[]{:S(2)}) %collective-permute-start.12) | collective-permute-done | bytes 1048608 | tf_op jit(solution)/shard_map/ppermute | solution.py:22
  236.4 1.3 fusion.15
  237.8 36.3 %collective-permute-start.13 = (f32[16,128,128]{2,1,0:T(8,128)}, f32[16,128,128]{2,1,0:T(8,128)}, u32[]{:S(2)}, u32[]{:S(2)}) collective-permute-start(f32[16,128,128]{2,1,0:T(8,128)} %fusion.15), channel_id=1, source_target_pairs={{0,16},{16,0},{1,17},{17,1},{2,18},{18,2},{3,19},{19,3},{4,20},{20... | collective-permute-start | bytes 3145736 | tf_op jit(solution)/shard_map/ppermute | solution.py:16
  275.1 2.1 fusion.57
  277.2 17.4 %collective-permute-done.13 = f32[16,128,128]{2,1,0:T(8,128)} collective-permute-done((f32[16,128,128]{2,1,0:T(8,128)}, f32[16,128,128]{2,1,0:T(8,128)}, u32[]{:S(2)}, u32[]{:S(2)}) %collective-permute-start.13) | collective-permute-done | bytes 1048608 | tf_op jit(solution)/shard_map/ppermute | solution.py:16
  294.6 2.0 fusion.14
  297.4 2.4 fusion.68
  300.1 17.7 %collective-permute-done.14 = f32[16,128,128]{2,1,0:T(8,128)S(1)} collective-permute-done((f32[16,128,128]{2,1,0:T(8,128)S(1)}, f32[16,128,128]{2,1,0:T(8,128)S(1)}, u32[]{:S(2)}, u32[]{:S(2)}) %collective-permute-start.14) | collective-permute-done | bytes 1048608 | tf_op jit(solution)/shard_map/ppermute | solution.py:16
  317.8 2.9 fusion.13
  320.8 7.7 %collective-permute-start.15 = (f32[16,128,128]{2,1,0:T(8,128)}, f32[16,128,128]{2,1,0:T(8,128)}, u32[]{:S(2)}, u32[]{:S(2)}) collective-permute-start(f32[16,128,128]{2,1,0:T(8,128)} %get-tuple-element.66), channel_id=1, source_target_pairs={{0,4},{4,0},{1,5},{5,1},{2,6},{6,2},{3,7},{7,3},{8,12},{12,8},{9,1... | collective-permute-start | bytes 3145736 | tf_op jit(solution)/shard_map/ppermute | solution.py:16
  328.6 2.3 convolution_bitcast_fusion.2
  330.9 2.0 fusion.42
  332.9 2.5 fusion.44
  335.4 1.3 collective-permute-start.18
  337.7 1.3 fusion.29
  339.1 11.8 %collective-permute-done.15 = f32[16,128,128]{2,1,0:T(8,128)} collective-permute-done((f32[16,128,128]{2,1,0:T(8,128)}, f32[16,128,128]{2,1,0:T(8,128)}, u32[]{:S(2)}, u32[]{:S(2)}) %collective-permute-start.15) | collective-permute-done | bytes 1048608 | tf_op jit(solution)/shard_map/ppermute | solution.py:16
  350.9 7.6 %multiply_reduce_fusion.1 = (f32[16]{0:T(128)S(1)}, f32[16]{0:T(128)S(1)}, f32[16]{0:T(128)S(1)}, f32[16]{0:T(128)S(1)}, f32[16]{0:T(128)S(1)}, /*index=5*/f32[1...) fusion(f32[16,128,128]{2,1,0:T(8,128)} %collective-permute-done, ...), kind=kLoop, calls=%fused_computation.71 | loop fusion | flops 8388384 | bytes 19923968 | tf_op jit(solution)/shard_map/reduce_sum | solution.py:97
  358.5 1.8 fusion.12
  360.4 1.6 collective-permute-start.16
  363.1 2.4 fusion.26
  365.5 11.5 %fusion.23 = bf16[16,128,128]{1,2,0:T(8,128)(2,1)} fusion(f32[16,128,128]{1,2,0:T(8,128)S(1)} %copy-done.15, f32[6,16,128,128]{3,2,1,0:T(8,128)S(1)} %bitcast.171, f32[16,128,128]{1,2,0:T(8,128)S(1)} %copy-done.10, f32[6,16,128]{2,0,1:T(8,128)S(1)} %copy.72), kind=kOutput, calls=%fused_computation.37 | convolution fusion | flops 2418016256 | bytes 8962048 | tf_op jit(solution)/shard_map/jvp(jhik,jhkv->hiv)/dot_general | solution.py:63
  376.9 6.7 %collective-permute-done.16 = f32[16,128,128]{2,1,0:T(8,128)S(1)} collective-permute-done((f32[16,128,128]{2,1,0:T(8,128)S(1)}, f32[16,128,128]{2,1,0:T(8,128)S(1)}, u32[]{:S(2)}, u32[]{:S(2)}) %collective-permute-start.16) | collective-permute-done | bytes 1048608 | tf_op jit(solution)/shard_map/ppermute | solution.py:16
  384.2 2.4 fusion.11
  386.6 2.8 collective-permute-start.17
  389.5 2.0 copy.86
  391.5 1.3 collective-permute-done.19
  392.9 1.2 reduce_window_sum.33
  395.3 2.8 collective-permute-start.21
  398.1 2.0 copy.87
  400.6 2.2 copy.90
  402.8 3.7 collective-permute-start.23
  406.5 2.6 fusion.30
  409.2 3.3 fusion.38
  412.4 2.0 copy.88
  414.6 3.6 fusion.27
  419.3 1.2 reduce_window_sum.34
  (109 shorter events, 15.1 us)
Async XLA Ops:
  4.9 88.3 %copy-start.5 = (f32[16,128,128]{2,1,0:T(8,128)}, f32[16,128,128]{2,1,0:T(8,128)S(1)}, u32[]{:S(2)}) copy-start(f32[16,128,128]{2,1,0:T(8,128)S(1)} %fusion.28) | copy-start | bytes 3145732
  4.9 5.6 %collective-permute-start = (f32[16,128,128]{2,1,0:T(8,128)S(1)}, f32[16,128,128]{2,1,0:T(8,128)S(1)}, u32[]{:S(2)}, u32[]{:S(2)}) collective-permute-start(f32[16,128,128]{2,1,0:T(8,128)S(1)} %fusion.28), channel_id=1, source_target_pairs={{0,1},{1,0},{2,3},{3,2},{4,5},{5,4},{6,7},{7,6},{8,9},{9,8},{10,11... | collective-permute-start | bytes 3145736 | tf_op jit(solution)/shard_map/ppermute | solution.py:16
  8.2 2.3 collective-permute-start.1
  10.5 136.4 %copy-start.7 = (f32[16,128,128]{2,1,0:T(8,128)}, f32[16,128,128]{2,1,0:T(8,128)S(1)}, u32[]{:S(2)}) copy-start(f32[16,128,128]{2,1,0:T(8,128)S(1)} %collective-permute-done) | copy-start | bytes 3145732
  10.5 84.3 %slice-start.2 = ((f32[14,16,128]{2,1,0:T(8,128)}), f32[6,16,128]{2,1,0:T(8,128)S(1)}, s32[]{:S(2)}) async-start(f32[14,16,128]{2,1,0:T(8,128)} %param.9), calls=%async_computation.2 | async-start | bytes 98304 | tf_op jit(solution)/shard_map/jvp()/slice | solution.py:62
  11.9 24.7 %collective-permute-start.2 = (f32[16,128,128]{2,1,0:T(8,128)}, f32[16,128,128]{2,1,0:T(8,128)}, u32[]{:S(2)}, u32[]{:S(2)}) collective-permute-start(f32[16,128,128]{2,1,0:T(8,128)} %select_add_fusion.4), channel_id=1, source_target_pairs={{0,2},{2,0},{1,3},{3,1},{4,6},{6,4},{5,7},{7,5},{8,10},{10,8},{9,1... | collective-permute-start | bytes 3145736 | tf_op jit(solution)/shard_map/ppermute | solution.py:16
  11.9 24.7 %collective-permute-start.3 = (f32[16]{0:T(128)S(1)}, f32[16]{0:T(128)S(1)}, u32[]{:S(2)}, u32[]{:S(2)}) collective-permute-start(f32[16]{0:T(128)S(1)} %get-tuple-element.87), channel_id=1, source_target_pairs={{0,2},{2,0},{1,3},{3,1},{4,6},{6,4},{5,7},{7,5},{8,10},{10,8},{9,1... | collective-permute-start | bytes 200 | tf_op jit(solution)/shard_map/ppermute | solution.py:16
  39.3 25.3 %collective-permute-start.4 = (f32[16,128,128]{2,1,0:T(8,128)}, f32[16,128,128]{2,1,0:T(8,128)}, u32[]{:S(2)}, u32[]{:S(2)}) collective-permute-start(f32[16,128,128]{2,1,0:T(8,128)} %select_add_fusion.3), channel_id=1, source_target_pairs={{0,4},{4,0},{1,5},{5,1},{2,6},{6,2},{3,7},{7,3},{8,12},{12,8},{9,1... | collective-permute-start | bytes 3145736 | tf_op jit(solution)/shard_map/ppermute | solution.py:16
  40.5 24.1 %collective-permute-start.5 = (f32[16]{0:T(128)S(1)}, f32[16]{0:T(128)S(1)}, u32[]{:S(2)}, u32[]{:S(2)}) collective-permute-start(f32[16]{0:T(128)S(1)} %get-tuple-element.85), channel_id=1, source_target_pairs={{0,4},{4,0},{1,5},{5,1},{2,6},{6,2},{3,7},{7,3},{8,12},{12,8},{9,1... | collective-permute-start | bytes 200 | tf_op jit(solution)/shard_map/ppermute | solution.py:16
  67.4 23.0 %collective-permute-start.6 = (f32[16,128,128]{2,1,0:T(8,128)}, f32[16,128,128]{2,1,0:T(8,128)}, u32[]{:S(2)}, u32[]{:S(2)}) collective-permute-start(f32[16,128,128]{2,1,0:T(8,128)} %select_add_fusion.2), channel_id=1, source_target_pairs={{0,8},{8,0},{1,9},{9,1},{2,10},{10,2},{3,11},{11,3},{4,12},{12,4},... | collective-permute-start | bytes 3145736 | tf_op jit(solution)/shard_map/ppermute | solution.py:16
  67.4 23.0 %collective-permute-start.7 = (f32[16]{0:T(128)S(1)}, f32[16]{0:T(128)S(1)}, u32[]{:S(2)}, u32[]{:S(2)}) collective-permute-start(f32[16]{0:T(128)S(1)} %get-tuple-element.84), channel_id=1, source_target_pairs={{0,8},{8,0},{1,9},{9,1},{2,10},{10,2},{3,11},{11,3},{4,12},{12,4},... | collective-permute-start | bytes 200 | tf_op jit(solution)/shard_map/ppermute | solution.py:16
  93.2 55.1 %collective-permute-start.8 = (f32[16,128,128]{2,1,0:T(8,128)}, f32[16,128,128]{2,1,0:T(8,128)}, u32[]{:S(2)}, u32[]{:S(2)}) collective-permute-start(f32[16,128,128]{2,1,0:T(8,128)} %select_add_fusion.1), channel_id=1, source_target_pairs={{0,16},{16,0},{1,17},{17,1},{2,18},{18,2},{3,19},{19,3},{4,20},{20... | collective-permute-start | bytes 3145736 | tf_op jit(solution)/shard_map/ppermute | solution.py:16
  97.3 44.4 %collective-permute-start.9 = (f32[16]{0:T(128)S(1)}, f32[16]{0:T(128)S(1)}, u32[]{:S(2)}, u32[]{:S(2)}) collective-permute-start(f32[16]{0:T(128)S(1)} %get-tuple-element.82), channel_id=1, source_target_pairs={{0,16},{16,0},{1,17},{17,1},{2,18},{18,2},{3,19},{19,3},{4,20},{20... | collective-permute-start | bytes 200 | tf_op jit(solution)/shard_map/ppermute | solution.py:16
  99.3 105.3 %copy-start.3 = (bf16[128,2048]{0,1:T(8,128)(2,1)}, bf16[128,2048]{0,1:T(8,128)(2,1)S(1)}, u32[]{:S(2)}) copy-start(bf16[128,2048]{0,1:T(8,128)(2,1)S(1)} %copy.107) | copy-start | bytes 1572868
  141.8 11.9 %collective-permute-start.11 = (f32[16]{0:T(128)S(1)}, f32[16]{0:T(128)S(1)}, u32[]{:S(2)}, u32[]{:S(2)}) collective-permute-start(f32[16]{0:T(128)S(1)} %get-tuple-element.79), channel_id=1, source_target_pairs={{0,32},{32,0},{1,33},{33,1},{2,34},{34,2},{3,35},{35,3},{4,36},{36... | collective-permute-start | bytes 200 | tf_op jit(solution)/shard_map/ppermute | solution.py:16
  148.3 50.7 %copy-start.9 = (f32[16,128,128]{1,2,0:T(8,128)S(1)}, f32[16,128,128]{1,2,0:T(8,128)}, u32[]{:S(2)}) copy-start(f32[16,128,128]{1,2,0:T(8,128)} %convert_multiply_fusion.3) | copy-start | bytes 3145732
  150.3 47.7 %collective-permute-start.10 = (f32[16,128,128]{2,1,0:T(8,128)S(1)}, f32[16,128,128]{2,1,0:T(8,128)S(1)}, u32[]{:S(2)}, u32[]{:S(2)}) collective-permute-start(f32[16,128,128]{2,1,0:T(8,128)S(1)} %get-tuple-element.64), channel_id=1, source_target_pairs={{0,32},{32,0},{1,33},{33,1},{2,34},{34,2},{3,35},{35,3},{4,36},{36... | collective-permute-start | bytes 3145736 | tf_op jit(solution)/shard_map/ppermute | solution.py:16
  198.1 1.0 copy-start.16
  199.1 5.5 %copy-start.1 = (f32[6,16,128,128]{3,2,1,0:T(8,128)}, f32[6,16,128,128]{3,2,1,0:T(8,128)S(1)}, u32[]{:S(2)}) copy-start(f32[6,16,128,128]{3,2,1,0:T(8,128)S(1)} %bitcast_dynamic-update-slice_fusion) | copy-start | bytes 18874372
  204.6 69.4 %slice-start.3 = ((f32[14,16,128]{2,1,0:T(8,128)}), f32[8,16,128]{2,1,0:T(8,128)S(1)}, s32[]{:S(2)}) async-start(f32[14,16,128]{2,1,0:T(8,128)} %param.9), calls=%async_computation.3 | async-start | bytes 131072 | tf_op jit(solution)/shard_map/jvp()/slice | solution.py:56
  207.6 28.8 %copy-start = (f32[6,16,128,128]{3,2,1,0:T(8,128)}, f32[6,16,128,128]{3,2,1,0:T(8,128)S(1)}, u32[]{:S(2)}) copy-start(f32[6,16,128,128]{3,2,1,0:T(8,128)S(1)} %fusion.8) | copy-start | bytes 18874372
  207.9 28.6 %collective-permute-start.12 = (f32[16,128,128]{2,1,0:T(8,128)S(1)}, f32[16,128,128]{2,1,0:T(8,128)S(1)}, u32[]{:S(2)}, u32[]{:S(2)}) collective-permute-start(f32[16,128,128]{2,1,0:T(8,128)S(1)} %add_select_fusion), channel_id=1, source_target_pairs={{32,0},{33,1},{34,2},{35,3},{36,4},{37,5},{38,6},{39,7},{40,8},{41... | collective-permute-start | bytes 3145736 | tf_op jit(solution)/shard_map/ppermute | solution.py:22
  236.4 60.9 %copy-start.13 = (f32[16,128,128]{2,1,0:T(8,128)}, f32[16,128,128]{2,1,0:T(8,128)S(1)}, u32[]{:S(2)}) copy-start(f32[16,128,128]{2,1,0:T(8,128)S(1)} %collective-permute-done.12) | copy-start | bytes 3145732
  237.8 56.9 %collective-permute-start.13 = (f32[16,128,128]{2,1,0:T(8,128)}, f32[16,128,128]{2,1,0:T(8,128)}, u32[]{:S(2)}, u32[]{:S(2)}) collective-permute-start(f32[16,128,128]{2,1,0:T(8,128)} %fusion.15), channel_id=1, source_target_pairs={{0,16},{16,0},{1,17},{17,1},{2,18},{18,2},{3,19},{19,3},{4,20},{20... | collective-permute-start | bytes 3145736 | tf_op jit(solution)/shard_map/ppermute | solution.py:16
  277.2 85.8 %copy-start.2 = (f32[128,128,16]{1,2,0:T(8,128)}, f32[128,128,16]{1,2,0:T(8,128)S(1)}, u32[]{:S(2)}) copy-start(f32[128,128,16]{1,2,0:T(8,128)S(1)} %fusion.57) | copy-start | bytes 3145732
  296.6 24.1 %copy-start.11 = (f32[16,128,128]{2,1,0:T(8,128)}, f32[16,128,128]{2,1,0:T(8,128)S(1)}, u32[]{:S(2)}) copy-start(f32[16,128,128]{2,1,0:T(8,128)S(1)} %get-tuple-element.69) | copy-start | bytes 3145732
  296.6 21.2 %collective-permute-start.14 = (f32[16,128,128]{2,1,0:T(8,128)S(1)}, f32[16,128,128]{2,1,0:T(8,128)S(1)}, u32[]{:S(2)}, u32[]{:S(2)}) collective-permute-start(f32[16,128,128]{2,1,0:T(8,128)S(1)} %get-tuple-element.68), channel_id=1, source_target_pairs={{0,8},{8,0},{1,9},{9,1},{2,10},{10,2},{3,11},{11,3},{4,12},{12,4},... | collective-permute-start | bytes 3145736 | tf_op jit(solution)/shard_map/ppermute | solution.py:16
  297.3 31.1 %copy-start.14 = (bf16[128,2048]{1,0:T(8,128)(2,1)S(1)}, bf16[128,2048]{1,0:T(8,128)(2,1)}, u32[]{:S(2)}) copy-start(bf16[128,2048]{1,0:T(8,128)(2,1)} %param.8) | copy-start | bytes 1572868
  299.7 31.2 %copy-start.4 = (bf16[128,2048]{0,1:T(8,128)(2,1)S(1)}, bf16[128,2048]{0,1:T(8,128)(2,1)}, u32[]{:S(2)}) copy-start(bf16[128,2048]{0,1:T(8,128)(2,1)} %copy-done.3) | copy-start | bytes 1572868
  320.8 30.2 %collective-permute-start.15 = (f32[16,128,128]{2,1,0:T(8,128)}, f32[16,128,128]{2,1,0:T(8,128)}, u32[]{:S(2)}, u32[]{:S(2)}) collective-permute-start(f32[16,128,128]{2,1,0:T(8,128)} %get-tuple-element.66), channel_id=1, source_target_pairs={{0,4},{4,0},{1,5},{5,1},{2,6},{6,2},{3,7},{7,3},{8,12},{12,8},{9,1... | collective-permute-start | bytes 3145736 | tf_op jit(solution)/shard_map/ppermute | solution.py:16
  335.4 53.9 %collective-permute-start.18 = (f32[16]{0:T(128)S(1)}, f32[16]{0:T(128)S(1)}, u32[]{:S(2)}, u32[]{:S(2)}) collective-permute-start(f32[16]{0:T(128)S(1)} %get-tuple-element.61), channel_id=1, source_target_pairs={{32,0},{33,1},{34,2},{35,3},{36,4},{37,5},{38,6},{39,7},{40,8},{41... | collective-permute-start | bytes 200 | tf_op jit(solution)/shard_map/ppermute | solution.py:22
  350.9 14.5 %slice-start = ((s8[6291456]{0:T(1024)(128)(4,1)}), s8[4194304]{0:T(1024)(128)(4,1)S(1)}, s32[]{:S(2)}) async-start(s8[6291456]{0:T(1024)(128)(4,1)} %bitcast.170), calls=%async_computation | async-start | bytes 8388608
  350.9 11.0 %copy-start.17 = (f32[8,16,128]{1,0,2:T(8,128)S(1)}, f32[8,16,128]{1,0,2:T(8,128)}, u32[]{:S(2)}) copy-start(f32[8,16,128]{1,0,2:T(8,128)} %convolution_bitcast_fusion.2) | copy-start | bytes 196612
  350.9 11.0 %copy-start.18 = (f32[6,16,128]{1,0,2:T(8,128)S(1)}, f32[6,16,128]{1,0,2:T(8,128)}, u32[]{:S(2)}) copy-start(f32[6,16,128]{1,0,2:T(8,128)} %copy.83) | copy-start | bytes 147460
  350.9 12.1 %copy-start.12 = (f32[16,128,128]{1,2,0:T(8,128)S(1)}, f32[16,128,128]{1,2,0:T(8,128)}, u32[]{:S(2)}) copy-start(f32[16,128,128]{1,2,0:T(8,128)} %get-tuple-element.30) | copy-start | bytes 3145732
  350.9 14.5 %slice-start.1 = ((s8[6291456]{0:T(1024)(128)(4,1)}), s8[2097152]{0:T(1024)(128)(4,1)S(1)}, s32[]{:S(2)}) async-start(s8[6291456]{0:T(1024)(128)(4,1)} %bitcast.170), calls=%async_computation.1 | async-start | bytes 4194304
  358.5 6.9 %copy-start.10 = (f32[16,128,128]{1,2,0:T(8,128)S(1)}, f32[16,128,128]{1,2,0:T(8,128)}, u32[]{:S(2)}) copy-start(f32[16,128,128]{1,2,0:T(8,128)} %convert_multiply_fusion.3) | copy-start | bytes 3145732
  358.5 6.9 %copy-start.15 = (f32[16,128,128]{1,2,0:T(8,128)S(1)}, f32[16,128,128]{1,2,0:T(8,128)}, u32[]{:S(2)}) copy-start(f32[16,128,128]{1,2,0:T(8,128)} %fusion.44) | copy-start | bytes 3145732
  360.4 23.3 %collective-permute-start.16 = (f32[16,128,128]{2,1,0:T(8,128)S(1)}, f32[16,128,128]{2,1,0:T(8,128)S(1)}, u32[]{:S(2)}, u32[]{:S(2)}) collective-permute-start(f32[16,128,128]{2,1,0:T(8,128)S(1)} %fusion.12), channel_id=1, source_target_pairs={{0,2},{2,0},{1,3},{3,1},{4,6},{6,4},{5,7},{7,5},{8,10},{10,8},{9,1... | collective-permute-start | bytes 3145736 | tf_op jit(solution)/shard_map/ppermute | solution.py:16
  363.0 20.6 %copy-start.6 = (f32[16,128,128]{2,1,0:T(8,128)S(1)}, f32[16,128,128]{2,1,0:T(8,128)}, u32[]{:S(2)}) copy-start(f32[16,128,128]{2,1,0:T(8,128)} %copy-done.5) | copy-start | bytes 3145732
  363.0 20.6 %copy-start.8 = (f32[16,128,128]{2,1,0:T(8,128)S(1)}, f32[16,128,128]{2,1,0:T(8,128)}, u32[]{:S(2)}) copy-start(f32[16,128,128]{2,1,0:T(8,128)} %copy-done.7) | copy-start | bytes 3145732
  386.6 20.0 %collective-permute-start.17 = (f32[16,128,128]{2,1,0:T(8,128)}, f32[16,128,128]{2,1,0:T(8,128)}, u32[]{:S(2)}, u32[]{:S(2)}) collective-permute-start(f32[16,128,128]{2,1,0:T(8,128)} %fusion.11), channel_id=1, source_target_pairs={{0,1},{1,0},{2,3},{3,2},{4,5},{5,4},{6,7},{7,6},{8,9},{9,8},{10,11... | collective-permute-start | bytes 3145736 | tf_op jit(solution)/shard_map/ppermute | solution.py:16
  389.4 3.4 collective-permute-start.19
  392.8 2.5 collective-permute-start.20
  395.3 4.8 %collective-permute-start.21 = (f32[16]{0:T(128)S(1)}, f32[16]{0:T(128)S(1)}, u32[]{:S(2)}, u32[]{:S(2)}) collective-permute-start(f32[16]{0:T(128)S(1)} %get-tuple-element.52), channel_id=1, source_target_pairs={{0,4},{4,0},{1,5},{5,1},{2,6},{6,2},{3,7},{7,3},{8,12},{12,8},{9,1... | collective-permute-start | bytes 200 | tf_op jit(solution)/shard_map/ppermute | solution.py:16
  400.1 2.7 collective-permute-start.22
  402.8 16.3 %collective-permute-start.23 = (f32[16]{0:T(128)S(1)}, f32[16]{0:T(128)S(1)}, u32[]{:S(2)}, u32[]{:S(2)}) collective-permute-start(f32[16]{0:T(128)S(1)} %get-tuple-element.46), channel_id=1, source_target_pairs={{0,1},{1,0},{2,3},{3,2},{4,5},{5,4},{6,7},{7,6},{8,9},{9,8},{10,11... | collective-permute-start | bytes 200 | tf_op jit(solution)/shard_map/ppermute | solution.py:16
where the time goes:
time: 429 us; the launch traced here: 421 us
  waiting for transfers between devices  238 us (55%)
  starting transfers between devices  75.6 us (18%)
  matrix products  45.2 us (11%)
  other arithmetic  44.5 us (10%)
  local copies, waits for them, and re-layouts  16.6 us (4%)
    ppermute x22, waiting for transfers between devices, from_partner(): return lax.ppermute(block, axis, route)  211 us
    ppermute x22, starting transfers between devices, from_partner(): return lax.ppermute(block, axis, route)  73.1 us
    ppermute x2, waiting for transfers between devices, passed_along(): lax.ppermute(value, axis, [(source, source + steps) for source in range(f...  27.3 us
    dot_general x3, matrix products, block_output(): jnp.einsum('jhik,jhkv->hiv', reach, buckets, precision=TOP_ACCURACY)  20 us
    unnamed x50, local copies, waits for them, and re-layouts  13 us
    select_n x6, other arithmetic, partner_grads(): jnp.where(is_upper, factor[:, None, None] * g_state + jnp.exp(offset)[:,...  10.7 us
    add x4, other arithmetic, merge_step(): merged = jnp.exp(high_total)[:, None, None] * low_state + high_state  9.66 us
  transfers between devices with their start and end apart: 24, of which 13 were waited for; matrix products, arithmetic and copies ran while one was open for 18% of the time, Pallas kernels for 0%

commit v1 on v0

v1 whole, which is shorter than its diff:
```python
import jax
import jax.numpy as jnp
from jax import lax
from jax.experimental import pallas as pl
from jax.experimental.pallas import tpu as pltpu
from jax.sharding import PartitionSpec as P

MESH = pl.DeviceIdType.MESH
F32 = jnp.float32
BF16 = jnp.bfloat16
H = 16
HH = 8
N = 128
NR = 136
LVL_IN = 8
XLEV = 6
GRAN = 2

NN = (((1,), (0,)), ((), ()))
NT = (((1,), (1,)), ((), ()))


def mm(a, b, dims=NN):
    return lax.dot_general(a, b, dims, preferred_element_type=F32)


def split(x):
    hi = x.astype(BF16)
    lo = (x - hi.astype(F32)).astype(BF16)
    return hi, lo


def wide(x):
    hi, lo = split(x)
    return jnp.concatenate([hi, lo], axis=1)


def tall(x):
    hi, lo = split(x)
    return jnp.concatenate([hi, lo], axis=0)


def flip(x):
    return jnp.transpose(x.astype(F32)).astype(BF16)


def running_sums(decay):
    r = lax.broadcasted_iota(jnp.int32, (N, N), 0)
    t = lax.broadcasted_iota(jnp.int32, (N, N), 1)
    upper = (r <= t).astype(F32)
    run = lax.dot_general(decay, upper, NN, precision=lax.Precision.HIGHEST, preferred_element_type=F32)
    tot = lax.dot_general(decay, jnp.ones((N, N), F32), NN, precision=lax.Precision.HIGHEST, preferred_element_type=F32)
    return run, tot


def front_kernel(q_ref, k_ref, v_ref, g_ref, gain_ref, decay_ref, s_ref, big_ref, run_sc, tot_sc):
    h = pl.program_id(0)

    @pl.when(h == 0)
    def _():
        run, tot = running_sums(decay_ref[...])
        run_sc[...] = run
        tot_sc[...] = tot

    run = run_sc[pl.ds(h, 1), :]
    tot = tot_sc[pl.ds(h, 1), :]
    v = v_ref[...]
    g = g_ref[...]
    kt = jnp.transpose(k_ref[...].astype(F32))
    qt = jnp.transpose(q_ref[...].astype(F32))
    vv = jnp.concatenate([v, v], axis=0)
    gg = jnp.concatenate([g, g], axis=0)
    s_ref[0, 0:N, :] = mm(wide(kt * jnp.exp(tot - run)), vv)
    s_ref[0, N:NR, :] = jnp.broadcast_to(tot, (NR - N, N))
    lift = jnp.exp(run)
    for j in range(XLEV):
        row = gain_ref[LVL_IN + j, pl.ds(h, 1), :] * lift
        big_ref[j, 0] = mm(wide(qt * row), gg)


def front(q, k, v, g, gain, decay):
    col = pl.BlockSpec((N, N), lambda h: (0, h))
    return pl.pallas_call(
        front_kernel,
        grid=(H,),
        in_specs=[col, col, col, col,
                  pl.BlockSpec((LVL_IN + XLEV, H, N), lambda h: (0, 0, 0)),
                  pl.BlockSpec((H, N), lambda h: (0, 0))],
        out_specs=[pl.BlockSpec((1, NR, N), lambda h: (h, 0, 0)),
                   pl.BlockSpec((XLEV, 1, N, N), lambda h: (0, h, 0, 0))],
        out_shape=[jax.ShapeDtypeStruct((H, NR, N), F32),
                   jax.ShapeDtypeStruct((XLEV, H, N, N), F32)],
        scratch_shapes=[pltpu.VMEM((H, N), F32), pltpu.VMEM((H, N), F32)],
        name="front",
    )(q, k, v, g, gain, decay)


def coords():
    c = lax.axis_index("ctx")
    return c, lax.rem(c, 2), lax.rem(c // 2, 4), c // 8


def comm_kernel(s_ref, g_ref, b0_ref, bk_ref, ds_ref,
                rg, cbuf, mbuf, rbuf, pbuf, qbuf, ebuf, fbuf, abuf, bbuf, ybuf, xbuf,
                ssem, rx1, rx2, ry1, ry2, rz, re, ra, rb, rlate):
    seq = lax.axis_index("seq")
    c, b, y, z = coords()
    mine = b * HH
    theirs = (1 - b) * HH
    part = c + 1 - 2 * b
    yn = c + 2 - 4 * lax.rem(y, 2)
    ym = c + 2 * (3 - 2 * y)
    up = c + 8
    dn = c - 8
    yodd = lax.rem(y, 2) == 1
    yhi = y >= 2
    zb = [lax.rem(z, 2) == 1, lax.rem(z // 2, 2) == 1, z >= 4]

    barrier = pltpu.get_barrier_semaphore()

    def greet(who):
        pl.semaphore_signal(barrier, inc=1, device_id=(seq, who), device_id_type=MESH)

    greet(part)
    greet(yn)
    greet(ym)

    @pl.when(z < 7)
    def _():
        greet(up)

    @pl.when(z > 0)
    def _():
        greet(dn)

    pl.semaphore_wait(barrier, 3 + jnp.minimum(z, 1) + jnp.minimum(7 - z, 1))

    def copy(src, dst, send, recv, who):
        return pltpu.make_async_remote_copy(src_ref=src, dst_ref=dst, send_sem=send, recv_sem=recv,
                                            device_id=(seq, who), device_id_type=MESH)

    def x1(h):
        return copy(s_ref.at[theirs + h], b0_ref.at[theirs + h], ssem.at[0], rx1.at[h], part)

    def x1b(h):
        return copy(s_ref.at[h], b0_ref.at[h], ssem.at[1], rlate.at[5], part)

    def x2(j, h):
        return copy(g_ref.at[j, theirs + h], rg.at[j, h], ssem.at[2 + j], rx2.at[j, h], part)

    def x4(j, h):
        return copy(bk_ref.at[j, mine + h], bk_ref.at[j, mine + h], ssem.at[8 + j], rlate.at[j], part)

    def x5(h):
        return copy(xbuf.at[h], ds_ref.at[mine + h], ssem.at[13], rlate.at[6], part)

    def y1(h):
        return copy(cbuf.at[h], bk_ref.at[0, mine + h], ssem.at[14], ry1.at[h], yn)

    def y2(h):
        return copy(mbuf.at[h], bk_ref.at[1, mine + h], ssem.at[15], ry2.at[h], ym)

    def zmsg(j, src, h):
        return copy(src, bk_ref.at[2 + j, mine + h], ssem.at[16 + j], rz.at[j, h], up)

    def emsg(j, h):
        return copy(fbuf.at[j, h], ebuf.at[j, h], ssem.at[19 + j], re.at[j, h], dn)

    def amsg(h):
        return copy(abuf.at[h], ybuf.at[0, h], ssem.at[22], ra.at[h], ym)

    def bmsg(h):
        return copy(bbuf.at[h], ybuf.at[1, h], ssem.at[23], rb.at[h], yn)

    setbits = [None, yodd, yhi, zb[0], zb[1], zb[2]]

    def tot(ref):
        return ref[N:N + 1, :]

    def each(fn):
        def body(h, carry):
            fn(h)
            return carry
        lax.fori_loop(0, HH, body, 0)

    each(lambda h: x1(h).start())

    def send_g(h):
        for j in (5, 4, 3, 2, 1):
            @pl.when(setbits[j])
            def _(j=j):
                x2(j, h).start()
    each(send_g)

    @pl.when(b == 0)
    def _():
        each(lambda h: x1b(h).start())

    @pl.when(b == 1)
    def _():
        each(lambda h: x2(0, h).start())

    @pl.when(z == 7)
    def _():
        def zero(h):
            ebuf[2, h] = jnp.zeros((N, N), F32)
        each(zero)

    def merge(out, low, high, ht):
        out[0:N, :] = jnp.exp(ht) * low[0:N, :] + high[0:N, :]
        out[N:NR, :] = low[N:NR, :] + high[N:NR, :]

    def f1(h):
        x1(h).wait_recv()

        @pl.when(b == 0)
        def _():
            merge(cbuf.at[h], s_ref.at[mine + h], b0_ref.at[mine + h], tot(b0_ref.at[mine + h]))

        @pl.when(b == 1)
        def _():
            merge(cbuf.at[h], b0_ref.at[mine + h], s_ref.at[mine + h], tot(s_ref.at[mine + h]))

        y1(h).start()

    def f2(h):
        y1(h).wait_recv()
        other = bk_ref.at[0, mine + h]

        @pl.when(yodd)
        def _():
            merge(mbuf.at[h], other, cbuf.at[h], tot(cbuf.at[h]))
            x4(0, h).start()

        @pl.when(jnp.logical_not(yodd))
        def _():
            merge(mbuf.at[h], cbuf.at[h], other, tot(other))

        y2(h).start()

    def f3(h):
        y2(h).wait_recv()
        other = bk_ref.at[1, mine + h]

        @pl.when(yhi)
        def _():
            merge(rbuf.at[h], other, mbuf.at[h], tot(mbuf.at[h]))
            x4(1, h).start()

        @pl.when(jnp.logical_not(yhi))
        def _():
            merge(rbuf.at[h], mbuf.at[h], other, tot(other))

        @pl.when(jnp.logical_not(zb[0]))
        def _():
            zmsg(0, rbuf.at[h], h).start()

    def f4(h):
        zmsg(0, rbuf.at[h], h).wait_recv()
        x4(2, h).start()
        merge(pbuf.at[h], bk_ref.at[2, mine + h], rbuf.at[h], tot(rbuf.at[h]))

        @pl.when(jnp.logical_not(zb[1]))
        def _():
            zmsg(1, pbuf.at[h], h).start()

    def f5(h):
        here = bk_ref.at[3, mine + h]
        zmsg(1, here, h).wait_recv()

        @pl.when(jnp.logical_not(zb[0]))
        def _():
            zmsg(1, here, h).start()

        x4(3, h).start()

        @pl.when(z == 3)
        def _():
            merge(qbuf.at[h], here, pbuf.at[h], tot(pbuf.at[h]))
            zmsg(2, qbuf.at[h], h).start()

    def f7(h):
        here = bk_ref.at[4, mine + h]
        zmsg(2, here, h).wait_recv()

        @pl.when(z < 7)
        def _():
            zmsg(2, here, h).start()

        x4(4, h).start()

    def base_tot(h):
        own = tot(s_ref.at[mine + h])
        other = tot(b0_ref.at[mine + h])
        return jnp.where(b == 0, own, other)

    def chip_grad(j, h, off):
        e0 = jnp.exp(base_tot(h))
        own = g_ref[j, mine + h]
        other = rg[j, h]
        low = jnp.where(b == 0, jnp.exp(off), e0 * jnp.exp(off))
        high = jnp.where(b == 0, e0 * jnp.exp(off), jnp.exp(off))
        return low * own + high * other

    def row_off(h):
        t1 = tot(bk_ref.at[0, mine + h])
        t2 = tot(bk_ref.at[1, mine + h])
        return jnp.where(yodd, t1, 0.0) + jnp.where(yhi, t2, 0.0)

    in_slot = [jnp.where(zb[1], 2, 1), jnp.where(zb[0], 2, 1), 2]
    d_slot = jnp.where(zb[0], jnp.where(zb[1], 2, 1), 0)

    def back(h):
        @pl.when(jnp.logical_not(zb[0]))
        def _():
            emsg(0, h).wait_recv()

        @pl.when(zb[0] != zb[1])
        def _():
            emsg(1, h).wait_recv()

        @pl.when(jnp.logical_and(z >= 3, z < 7))
        def _():
            emsg(2, h).wait_recv()

        off = row_off(h)
        ez = jnp.exp(tot(rbuf.at[h]))
        for j in (2, 1, 0):
            @pl.when(zb[j])
            def _(j=j):
                x2(3 + j, h).wait_recv()
                fbuf[j, h] = ez * ebuf[in_slot[j], h] + chip_grad(3 + j, h, off)
                emsg(j, h).start()

        @pl.when(yhi)
        def _():
            x2(2, h).wait_recv()
            e23 = jnp.exp(tot(mbuf.at[h]))
            off2 = jnp.where(yodd, tot(bk_ref.at[0, mine + h]), 0.0)
            abuf[h] = e23 * ebuf[d_slot, h] + chip_grad(2, h, off2)

        @pl.when(jnp.logical_not(yhi))
        def _():
            abuf[h] = ebuf[d_slot, h]

        amsg(h).start()

    def ya(h):
        amsg(h).wait_recv()
        e23 = jnp.where(yhi, 1.0, jnp.exp(tot(bk_ref.at[1, mine + h])))
        yv = e23 * ebuf[d_slot, h] + ybuf[0, h]
        ybuf[2, h] = yv

        @pl.when(yodd)
        def _():
            x2(1, h).wait_recv()
            bbuf[h] = jnp.exp(tot(cbuf.at[h])) * yv + chip_grad(1, h, jnp.zeros((1, N), F32))

        @pl.when(jnp.logical_not(yodd))
        def _():
            bbuf[h] = yv

        bmsg(h).start()

    def yb(h):
        bmsg(h).wait_recv()
        e1 = jnp.where(yodd, 1.0, jnp.exp(tot(bk_ref.at[0, mine + h])))
        dc = e1 * ybuf[2, h] + ybuf[1, h]

        @pl.when(b == 0)
        def _():
            x2(0, h).wait_recv()
            ds_ref[mine + h] = jnp.exp(tot(b0_ref.at[mine + h])) * dc + rg[0, h]
            xbuf[h] = dc

        @pl.when(b == 1)
        def _():
            ds_ref[mine + h] = dc
            xbuf[h] = jnp.exp(tot(s_ref.at[mine + h])) * dc + g_ref[0, mine + h]

        x5(h).start()

    d = GRAN
    back0 = 2 * d

    def tick(t, carry):
        def stage(fn, lag, cond=None):
            h = t - lag
            ok = jnp.logical_and(h >= 0, h < HH)
            if cond is not None:
                ok = jnp.logical_and(ok, cond)

            @pl.when(ok)
            def _():
                fn(h)

        stage(f1, 0)
        stage(f2, d)
        stage(f3, 2 * d)
        stage(back, back0 + (7 - z) * d)
        stage(f4, 3 * d, zb[0])
        stage(f5, 4 * d + jnp.where(zb[0], d, 0), zb[1])
        stage(f7, 6 * d + (z - 4) * d, zb[2])
        stage(ya, back0 + (8 - z) * d)
        stage(yb, back0 + (9 - z) * d)
        return carry

    lax.fori_loop(0, HH + back0 + 9 * d, tick, 0)

    def all_of(src, dst, send, recv):
        return copy(src, dst, send, recv, part)

    half = pl.ds(0, HH)
    for j in range(5):
        def late(j=j):
            all_of(bk_ref.at[j, half], bk_ref.at[j, half], ssem.at[8 + j], rlate.at[j]).wait()
        pl.when(setbits[j + 1])(late)
        def sent(j=j):
            all_of(rg.at[j, half], rg.at[j, half], ssem.at[3 + j], rlate.at[j]).wait_send()
        pl.when(setbits[j + 1])(sent)

    @pl.when(b == 0)
    def _():
        all_of(s_ref.at[half], s_ref.at[half], ssem.at[1], rlate.at[5]).wait_send()

    @pl.when(b == 1)
    def _():
        all_of(s_ref.at[half], s_ref.at[half], ssem.at[1], rlate.at[5]).wait_recv()
        all_of(rg.at[0, half], rg.at[0, half], ssem.at[2], rlate.at[5]).wait_send()

    all_of(xbuf.at[half], xbuf.at[half], ssem.at[13], rlate.at[6]).wait()
    all_of(s_ref.at[half], s_ref.at[half], ssem.at[0], rlate.at[5]).wait_send()
    all_of(cbuf.at[half], cbuf.at[half], ssem.at[14], rlate.at[5]).wait_send()
    all_of(mbuf.at[half], mbuf.at[half], ssem.at[15], rlate.at[5]).wait_send()
    all_of(abuf.at[half], abuf.at[half], ssem.at[22], rlate.at[5]).wait_send()
    all_of(bbuf.at[half], bbuf.at[half], ssem.at[23], rlate.at[5]).wait_send()
    out_cond = [jnp.logical_not(zb[0]), zb[0] != zb[1], jnp.logical_and(z >= 3, z < 7)]
    for j in range(3):
        def zsent(j=j):
            all_of(cbuf.at[half], cbuf.at[half], ssem.at[16 + j], rlate.at[5]).wait_send()
        pl.when(out_cond[j])(zsent)
        def esent(j=j):
            all_of(fbuf.at[j, half], fbuf.at[j, half], ssem.at[19 + j], rlate.at[5]).wait_send()
        pl.when(zb[j])(esent)


def comm(s, big):
    vm = pl.BlockSpec(memory_space=pltpu.VMEM)
    st = lambda *lead: pltpu.VMEM(lead + (NR, N), F32)
    sg = lambda *lead: pltpu.VMEM(lead + (N, N), F32)
    dma = pltpu.SemaphoreType.DMA
    return pl.pallas_call(
        comm_kernel,
        in_specs=[vm, vm],
        out_specs=[vm, vm, vm],
        out_shape=[jax.ShapeDtypeStruct((H, NR, N), F32),
                   jax.ShapeDtypeStruct((XLEV - 1, H, NR, N), F32),
                   jax.ShapeDtypeStruct((H, N, N), F32)],
        scratch_shapes=[sg(6, HH), st(HH), st(HH), st(HH), st(HH), st(HH),
                        sg(3, HH), sg(3, HH), sg(HH), sg(HH), sg(3, HH), sg(HH),
                        dma((24,)), dma((HH,)), dma((6, HH)), dma((HH,)), dma((HH,)),
                        dma((3, HH)), dma((3, HH)), dma((HH,)), dma((HH,)), dma((7,))],
        compiler_params=pltpu.CompilerParams(collective_id=0, has_side_effects=True,
                                             vmem_limit_bytes=62 * 1024 * 1024),
        name="states",
    )(s, big)


def final_kernel(q_ref, k_ref, v_ref, g_ref, gain_ref, decay_ref, b0_ref, bk_ref, ds_ref,
                 o_ref, dq_ref, dk_ref, dv_ref, dgain_ref, rev_ref, tot_ref,
                 run_sc, tot_sc, row_sc, col_sc):
    h = pl.program_id(0)
    c = lax.axis_index("ctx")

    @pl.when(h == 0)
    def _():
        run, tot = running_sums(decay_ref[...])
        run_sc[...] = run
        tot_sc[...] = tot
        col_sc[...] = jnp.zeros((N, N), F32)

    run = run_sc[pl.ds(h, 1), :]
    tot = tot_sc[pl.ds(h, 1), :]
    q, k, v, g = q_ref[...], k_ref[...], v_ref[...], g_ref[...]
    qt32 = jnp.transpose(q.astype(F32))
    qt = qt32.astype(BF16)
    gt, kt, vt = flip(g), flip(k), flip(v)

    bits = [lax.rem(c // (1 << j), 2) == 1 for j in range(XLEV)]
    rows = []
    lifts = []
    off = run
    buckets = []
    for j in range(XLEV):
        src = b0_ref.at[0] if j == 0 else bk_ref.at[j - 1, 0]
        buckets.append(jnp.where(bits[j], src[0:N, :], 0.0))
        lift = jnp.where(bits[j], jnp.exp(off), 0.0)
        lifts.append(lift)
        rows.append(gain_ref[LVL_IN + j, pl.ds(h, 1), :] * lift)
        off = off + jnp.where(bits[j], src[N:N + 1, :], 0.0)
    rows += [run, jnp.exp(tot - run)]
    cols = jnp.transpose(jnp.concatenate(rows + [jnp.zeros((N - 8, N), F32)], axis=0))
    run_col = cols[:, 6:7]
    tail_col = cols[:, 7:8]

    s_i = lax.broadcasted_iota(jnp.int32, (N, N), 0)
    t_i = lax.broadcasted_iota(jnp.int32, (N, N), 1)
    causal = s_i <= t_i
    mixing = jnp.bitwise_xor(s_i, t_i)
    fade = jnp.where(causal, jnp.exp(jnp.where(causal, run - run_col, 0.0)), 0.0)
    weight = jnp.broadcast_to(gain_ref[0, pl.ds(h, 1), :], (N, N))
    for lev in range(1, LVL_IN):
        weight = jnp.where(mixing >= (1 << (lev - 1)), gain_ref[lev, pl.ds(h, 1), :], weight)
    sc = mm(k, qt)
    gv = mm(v, gt)
    wd = weight * fade
    wt = sc * wd
    xt = gv * wd
    pair = sc * gv * fade
    above = [jnp.sum(pair, axis=0, keepdims=True)]
    for lev in range(1, LVL_IN):
        above.append(jnp.sum(jnp.where(mixing >= (1 << (lev - 1)), pair, 0.0), axis=0, keepdims=True))
    above.append(jnp.zeros((1, N), F32))
    for lev in range(LVL_IN):
        dgain_ref[lev, pl.ds(h, 1), :] = above[lev] - above[lev + 1]

    vt2 = jnp.concatenate([vt, vt], axis=1)
    kt2 = jnp.concatenate([kt, kt], axis=1)
    gt2 = jnp.concatenate([gt, gt], axis=0)
    q2 = jnp.concatenate([q, q], axis=1)
    o = jnp.transpose(mm(vt2, tall(wt)))
    dqt = mm(kt2, tall(xt))
    for j in range(XLEV):
        m_hi, m_lo = split(buckets[j])
        o = o + cols[:, j:j + 1] * mm(q2, jnp.concatenate([m_hi, m_lo], axis=0))
        dt = mm(jnp.concatenate([m_hi, m_lo], axis=1), gt2)
        dqt = dqt + rows[j] * dt
        dgain_ref[LVL_IN + j, pl.ds(h, 1), :] = lifts[j] * jnp.sum(dt * qt32, axis=0, keepdims=True)
    o_ref[...] = o.astype(BF16)
    dq_ref[...] = jnp.transpose(dqt).astype(BF16)
    row_sc[pl.ds(h, 1), :] = jnp.sum(dqt * qt32, axis=0, keepdims=True)

    d_hi, d_lo = split(ds_ref[0])
    k2 = jnp.concatenate([k, k], axis=1)
    v2 = jnp.concatenate([v, v], axis=1)
    dv = mm(wide(wt), jnp.concatenate([g, g], axis=0))
    dv = dv + tail_col * mm(k2, jnp.concatenate([d_hi, d_lo], axis=0))
    dk = mm(wide(xt), jnp.concatenate([q, q], axis=0))
    dk = dk + tail_col * mm(v2, jnp.concatenate([d_hi, d_lo], axis=1), NT)
    dk_ref[...] = dk.astype(BF16)
    dv_ref[...] = dv.astype(BF16)
    col = jnp.sum(v.astype(F32) * dv, axis=1, keepdims=True)
    col_sc[...] = jnp.where(t_i == h, col, col_sc[...])

    @pl.when(h == H - 1)
    def _():
        da = row_sc[...] - jnp.transpose(col_sc[...])[0:H, :]
        lower = (s_i >= t_i).astype(F32)
        rev_ref[...] = lax.dot_general(da, lower, NN, precision=lax.Precision.HIGHEST, preferred_element_type=F32)
        tot_ref[...] = lax.dot_general(da, jnp.ones((N, N), F32), NN, precision=lax.Precision.HIGHEST,
                                       preferred_element_type=F32)


def final(q, k, v, g, gain, decay, b0, bk, ds):
    col = pl.BlockSpec((N, N), lambda h: (0, h))
    whole3 = pl.BlockSpec((LVL_IN + XLEV, H, N), lambda h: (0, 0, 0))
    whole2 = pl.BlockSpec((H, N), lambda h: (0, 0))
    wide_out = jax.ShapeDtypeStruct((N, H * N), BF16)
    return pl.pallas_call(
        final_kernel,
        grid=(H,),
        in_specs=[col, col, col, col, whole3, whole2,
                  pl.BlockSpec((1, NR, N), lambda h: (h, 0, 0)),
                  pl.BlockSpec((XLEV - 1, 1, NR, N), lambda h: (0, h, 0, 0)),
                  pl.BlockSpec((1, N, N), lambda h: (h, 0, 0))],
        out_specs=[col, col, col, col, whole3, whole2, whole2],
        out_shape=[wide_out, wide_out, wide_out, wide_out,
                   jax.ShapeDtypeStruct((LVL_IN + XLEV, H, N), F32),
                   jax.ShapeDtypeStruct((H, N), F32), jax.ShapeDtypeStruct((H, N), F32)],
        scratch_shapes=[pltpu.VMEM((H, N), F32), pltpu.VMEM((H, N), F32),
                        pltpu.VMEM((H, N), F32), pltpu.VMEM((N, N), F32)],
        name="final",
    )(q, k, v, g, gain, decay, b0, bk, ds)


def suffix_kernel(rev_ref, tot_ref, out_ref, rowin, zin, sendbuf, ssem, rsem, zssem, zrsem):
    seq = lax.axis_index("seq")
    c, _, _, z = coords()
    r = lax.rem(c, 8)
    barrier = pltpu.get_barrier_semaphore()
    for i in range(1, 8):
        pl.semaphore_signal(barrier, inc=1, device_id=(seq, z * 8 + lax.rem(r + i, 8)), device_id_type=MESH)
        pl.semaphore_signal(barrier, inc=1, device_id=(seq, lax.rem(z + i, 8) * 8 + r), device_id_type=MESH)
    pl.semaphore_wait(barrier, 14)

    def rcopy(i):
        return pltpu.make_async_remote_copy(
            src_ref=tot_ref, dst_ref=rowin.at[i], send_sem=ssem.at[i], recv_sem=rsem.at[i],
            device_id=(seq, z * 8 + lax.rem(r + i, 8)), device_id_type=MESH)

    def zcopy(i):
        return pltpu.make_async_remote_copy(
            src_ref=sendbuf, dst_ref=zin.at[i], send_sem=zssem.at[i], recv_sem=zrsem.at[i],
            device_id=(seq, lax.rem(z + i, 8) * 8 + r), device_id_type=MESH)

    for i in range(1, 8):
        rcopy(i).start()
    total = tot_ref[...]
    after = jnp.zeros((H, N), F32)
    for i in range(1, 8):
        rcopy(i).wait_recv()
        val = rowin[i]
        total = total + val
        after = after + jnp.where(r - i < 0, val, 0.0)
    sendbuf[...] = total
    for i in range(1, 8):
        zcopy(i).start()
    acc = rev_ref[...] + after
    for i in range(1, 8):
        zcopy(i).wait_recv()
        acc = acc + jnp.where(z - i < 0, zin[i], 0.0)
    out_ref[...] = acc
    for i in range(1, 8):
        rcopy(i).wait_send()
        zcopy(i).wait_send()


def suffix(rev, tot):
    vm = pl.BlockSpec(memory_space=pltpu.VMEM)
    dma = pltpu.SemaphoreType.DMA
    return pl.pallas_call(
        suffix_kernel,
        in_specs=[vm, vm],
        out_specs=vm,
        out_shape=jax.ShapeDtypeStruct((H, N), F32),
        scratch_shapes=[pltpu.VMEM((8, H, N), F32), pltpu.VMEM((8, H, N), F32), pltpu.VMEM((H, N), F32),
                        dma((8,)), dma((8,)), dma((8,)), dma((8,))],
        compiler_params=pltpu.CompilerParams(collective_id=1, has_side_effects=True),
        name="suffix",
    )(rev, tot)


def per_device(queries, keys_in, value_input, level_gain, decay_log, out_grad):
    s, big = front(queries, keys_in, value_input, out_grad, level_gain, decay_log)
    b0, bk, ds = comm(s, big)
    o, dq, dk, dv, dgain, rev, tot = final(queries, keys_in, value_input, out_grad, level_gain, decay_log, b0, bk, ds)
    return o, dq, dk, dv, dgain, suffix(rev, tot)


def solution(mesh):
    tokens = P(("seq", "ctx"), None)
    gains = P(None, None, ("seq", "ctx"))
    decays = P(None, ("seq", "ctx"))
    return jax.shard_map(
        per_device,
        mesh=mesh,
        in_specs=(tokens, tokens, tokens, gains, decays, tokens),
        out_specs=(tokens, tokens, tokens, tokens, gains, decays),
        check_vma=False,
    )
```

time: 429 us -> 137 us (0.32); the launches traced: 421 us -> 136 us
  waiting for transfers between devices: 238 us -> 0 us
  Pallas kernels: 0 us -> 134 us
  starting transfers between devices: 75.6 us -> 0 us
  matrix products: 45.2 us -> 0 us
  other arithmetic: 44.5 us -> 0 us
  local copies, waits for them, and re-layouts: 16.6 us -> 1.3 us
    ppermute x24 -> x0, waiting for transfers between devices: 238 us -> none  [the longest x22 211 us: from_partner(): return lax.ppermute(block, axis, route)]
    pallas_call x0 -> x4, Pallas kernels: none -> 134 us  [the longest x1 90.1 us: comm(): pl.pallas_call(comm_kernel, in_specs=[vm, vm], out_specs=[vm, vm, vm], ou...]
    ppermute x24 -> x0, starting transfers between devices: 75.6 us -> none  [the longest x22 73.1 us: from_partner(): return lax.ppermute(block, axis, route)]
    dot_general x14 -> x0, matrix products: 45.2 us -> none  [the longest x3 20 us: block_output(): jnp.einsum('jhik,jhkv->hiv', reach, buckets, precision=TOP_ACCURACY)]
    unnamed x50 -> x1, local copies, waits for them, and re-layouts: 13 us -> 1.3 us
    reduce_sum x5 -> x0, other arithmetic: 11.5 us -> none  [the longest x1 7.57 us: own_grads(): jnp.sum(g_bucket * other_state, axis=(1, 2))]
    select_n x8 -> x0, other arithmetic: 10.7 us -> none  [the longest x6 10.7 us: partner_grads(): jnp.where(is_upper, factor[:, None, None] * g_state + jnp.exp(offset)[:,...]
    add x14 -> x0, other arithmetic: 10.4 us -> none  [the longest x4 9.66 us: merge_step(): merged = jnp.exp(high_total)[:, None, None] * low_state + high_state]
  transfers between devices with their start and end apart: 24 -> 0, of which waited for: 13 -> 0; matrix products, arithmetic and copies ran while one was open for 18% -> 0% of each run, Pallas kernels for 0% -> 0%
where the time goes in v1:
time: 137 us; the launch traced here: 136 us
  Pallas kernels  134 us (98%)
    pallas_call x1, Pallas kernels, comm(): pl.pallas_call(comm_kernel, in_specs=[vm, vm], out_specs=[vm, vm, vm], ou...  90.1 us
    pallas_call x1, Pallas kernels, final(): pl.pallas_call(final_kernel, grid=(H,), in_specs=[col, col, col, col, who...  18.1 us
    pallas_call x1, Pallas kernels, suffix(): pl.pallas_call(suffix_kernel, in_specs=[vm, vm], out_specs=vm, out_shape=...  13.3 us
    pallas_call x1, Pallas kernels, front(): pl.pallas_call(front_kernel, grid=(H,), in_specs=[col, col, col, col, pl....  12.2 us

profile of v1, /device:TPU:1, one launch (start us, length us, event | category | flops | bytes accessed | tf_op | source)
XLA Modules:
  0.0 135.8 jit_solution(11878862172296308973)
XLA Ops:
  0.6 12.2 %front.1 = (f32[16,136,128]{2,1,0:T(8,128)}, f32[6,16,128,128]{3,2,1,0:T(8,128)}) custom-call(bf16[128,2048]{1,0:T(8,128)(2,1)} %q_ref.3, bf16[128,2048]{1,0:T(8,128)(2,1)} %k_ref.3, bf16[128,2048]{1,0:T(8,128)(2,1)} %v_ref.3, bf16[128,2048]{1,0:T(8,128)(2,1)} %g_ref.3, f32[14,16,128]{2,1,0:T(8,128)} %gain_ref.3, f32[16,128]{1,0:T(8,128)} %decay_ref.3), custom_call_target="tpu_custom_call" | custom-call | tf_op jit(solution)/shard_map/front/pallas_call | solution.py:83
  12.9 90.1 %states.1 = (f32[16,136,128]{2,1,0:T(8,128)}, f32[5,16,136,128]{3,2,1,0:T(8,128)}, f32[16,128,128]{2,1,0:T(8,128)}) custom-call(f32[16,136,128]{2,1,0:T(8,128)} %get-tuple-element.18.s_ref, f32[6,16,128,128]{3,2,1,0:T(8,128)} %get-tuple-element.19.g_ref), custom_call_target="tpu_custom_call" | custom-call | tf_op jit(solution)/shard_map/states/pallas_call | solution.py:452
  103.0 18.1 %final.1 = (bf16[128,2048]{1,0:T(8,128)(2,1)}, bf16[128,2048]{1,0:T(8,128)(2,1)}, bf16[128,2048]{1,0:T(8,128)(2,1)}, bf16[128,2048]{1,0:T(8,128)(2,1)}, f32[14,1...) custom-call(bf16[128,2048]{1,0:T(8,128)(2,1)} %q_ref.3, bf16[128,2048]{1,0:T(8,128)(2,1)} %k_ref.3, ...), custom_call_target="tpu_custom_call" | custom-call | tf_op jit(solution)/shard_map/final/pallas_call | solution.py:569
  121.2 13.3 %suffix.1 = f32[16,128]{1,0:T(8,128)} custom-call(f32[16,128]{1,0:T(8,128)} %get-tuple-element.28.rev_ref, f32[16,128]{1,0:T(8,128)} %get-tuple-element.29.tot_ref), custom_call_target="tpu_custom_call" | custom-call | tf_op jit(solution)/shard_map/suffix/pallas_call | solution.py:631
  134.5 1.3 copy.13

commit v2 on v1

--- a/solution.py
+++ b/solution.py
@@ -11,7 +11,6 @@
 H = 16
 HH = 8
 N = 128
-NR = 136
 LVL_IN = 8
 XLEV = 6
 GRAN = 2
@@ -53,7 +52,7 @@
     return run, tot
 
 
-def front_kernel(q_ref, k_ref, v_ref, g_ref, gain_ref, decay_ref, s_ref, big_ref, run_sc, tot_sc):
+def front_kernel(q_ref, k_ref, v_ref, g_ref, gain_ref, decay_ref, s_ref, big_ref, own_ref, run_sc, tot_sc):
     h = pl.program_id(0)
 
     @pl.when(h == 0)
@@ -61,6 +60,7 @@
         run, tot = running_sums(decay_ref[...])
         run_sc[...] = run
         tot_sc[...] = tot
+        own_ref[...] = tot
 
     run = run_sc[pl.ds(h, 1), :]
     tot = tot_sc[pl.ds(h, 1), :]
@@ -70,8 +70,7 @@
     qt = jnp.transpose(q_ref[...].astype(F32))
     vv = jnp.concatenate([v, v], axis=0)
     gg = jnp.concatenate([g, g], axis=0)
-    s_ref[0, 0:N, :] = mm(wide(kt * jnp.exp(tot - run)), vv)
-    s_ref[0, N:NR, :] = jnp.broadcast_to(tot, (NR - N, N))
+    s_ref[0] = mm(wide(kt * jnp.exp(tot - run)), vv)
     lift = jnp.exp(run)
     for j in range(XLEV):
         row = gain_ref[LVL_IN + j, pl.ds(h, 1), :] * lift
@@ -86,10 +85,12 @@
         in_specs=[col, col, col, col,
                   pl.BlockSpec((LVL_IN + XLEV, H, N), lambda h: (0, 0, 0)),
                   pl.BlockSpec((H, N), lambda h: (0, 0))],
-        out_specs=[pl.BlockSpec((1, NR, N), lambda h: (h, 0, 0)),
-                   pl.BlockSpec((XLEV, 1, N, N), lambda h: (0, h, 0, 0))],
-        out_shape=[jax.ShapeDtypeStruct((H, NR, N), F32),
-                   jax.ShapeDtypeStruct((XLEV, H, N, N), F32)],
+        out_specs=[pl.BlockSpec((1, N, N), lambda h: (h, 0, 0)),
+                   pl.BlockSpec((XLEV, 1, N, N), lambda h: (0, h, 0, 0)),
+                   pl.BlockSpec((H, N), lambda h: (0, 0))],
+        out_shape=[jax.ShapeDtypeStruct((H, N, N), F32),
+                   jax.ShapeDtypeStruct((XLEV, H, N, N), F32),
+                   jax.ShapeDtypeStruct((H, N), F32)],
         scratch_shapes=[pltpu.VMEM((H, N), F32), pltpu.VMEM((H, N), F32)],
         name="front",
     )(q, k, v, g, gain, decay)
@@ -100,11 +101,19 @@
     return c, lax.rem(c, 2), lax.rem(c // 2, 4), c // 8
 
 
-def comm_kernel(s_ref, g_ref, b0_ref, bk_ref, ds_ref,
-                rg, cbuf, mbuf, rbuf, pbuf, qbuf, ebuf, fbuf, abuf, bbuf, ybuf, xbuf,
-                ssem, rx1, rx2, ry1, ry2, rz, re, ra, rb, rlate):
+def pick(parts, cond):
+    acc = jnp.zeros((H, N), F32)
+    for i in range(8):
+        acc = acc + jnp.where(cond(i), parts[i], 0.0)
+    return acc
+
+
+def comm_kernel(s_ref, g_ref, own_ref, b0_ref, bk_ref, ds_ref, off_ref,
+                rg, cbuf, mbuf, rbuf, pbuf, qbuf, ebuf, fbuf, abuf, bbuf, ybuf, xbuf, tt, rowt, zt, rsum,
+                ssem, rx1, rx2, ry1, ry2, rz, re, ra, rb, rlate, trs, trr, tzs, tzr):
     seq = lax.axis_index("seq")
     c, b, y, z = coords()
+    r = lax.rem(c, 8)
     mine = b * HH
     theirs = (1 - b) * HH
     part = c + 1 - 2 * b
@@ -115,25 +124,16 @@
     yodd = lax.rem(y, 2) == 1
     yhi = y >= 2
     zb = [lax.rem(z, 2) == 1, lax.rem(z // 2, 2) == 1, z >= 4]
+    row_peer = [z * 8 + lax.rem(r + i, 8) for i in range(8)]
+    z_peer = [lax.rem(z + i, 8) * 8 + r for i in range(8)]
+    row_from = [lax.rem(r - i + 8, 8) for i in range(8)]
+    z_from = [lax.rem(z - i + 8, 8) for i in range(8)]
 
     barrier = pltpu.get_barrier_semaphore()
-
-    def greet(who):
-        pl.semaphore_signal(barrier, inc=1, device_id=(seq, who), device_id_type=MESH)
-
-    greet(part)
-    greet(yn)
-    greet(ym)
-
-    @pl.when(z < 7)
-    def _():
-        greet(up)
-
-    @pl.when(z > 0)
-    def _():
-        greet(dn)
-
-    pl.semaphore_wait(barrier, 3 + jnp.minimum(z, 1) + jnp.minimum(7 - z, 1))
+    for i in range(1, 8):
+        pl.semaphore_signal(barrier, inc=1, device_id=(seq, row_peer[i]), device_id_type=MESH)
+        pl.semaphore_signal(barrier, inc=1, device_id=(seq, z_peer[i]), device_id_type=MESH)
+    pl.semaphore_wait(barrier, 14)
 
     def copy(src, dst, send, recv, who):
         return pltpu.make_async_remote_copy(src_ref=src, dst_ref=dst, send_sem=send, recv_sem=recv,
@@ -172,10 +172,13 @@
     def bmsg(h):
         return copy(bbuf.at[h], ybuf.at[1, h], ssem.at[23], rb.at[h], yn)
 
+    def rtot(i):
+        return copy(own_ref, rowt.at[i], trs.at[i], trr.at[i], row_peer[i])
+
+    def ztot(i):
+        return copy(rsum, zt.at[i], tzs.at[i], tzr.at[i], z_peer[i])
+
     setbits = [None, yodd, yhi, zb[0], zb[1], zb[2]]
-
-    def tot(ref):
-        return ref[N:N + 1, :]
 
     def each(fn):
         def body(h, carry):
@@ -183,14 +186,13 @@
             return carry
         lax.fori_loop(0, HH, body, 0)
 
+    for i in range(1, 8):
+        rtot(i).start()
     each(lambda h: x1(h).start())
-
-    def send_g(h):
-        for j in (5, 4, 3, 2, 1):
-            @pl.when(setbits[j])
-            def _(j=j):
-                x2(j, h).start()
-    each(send_g)
+    for j in (5, 4, 3, 2, 1):
+        @pl.when(setbits[j])
+        def _(j=j):
+            each(lambda h: x2(j, h).start())
 
     @pl.when(b == 0)
     def _():
@@ -206,20 +208,54 @@
             ebuf[2, h] = jnp.zeros((N, N), F32)
         each(zero)
 
-    def merge(out, low, high, ht):
-        out[0:N, :] = jnp.exp(ht) * low[0:N, :] + high[0:N, :]
-        out[N:NR, :] = low[N:NR, :] + high[N:NR, :]
+    for i in range(1, 8):
+        rtot(i).wait_recv()
+    parts = [own_ref[...]] + [rowt[i] for i in range(1, 8)]
+    rows = pick(parts, lambda i: row_from[i] >= 0)
+    rsum[...] = rows
+    for i in range(1, 8):
+        ztot(i).start()
+    core0 = pick(parts, lambda i: row_from[i] == 2 * y)
+    core1 = pick(parts, lambda i: row_from[i] == 2 * y + 1)
+    tt[0] = core0
+    tt[1] = core1
+    tt[2] = pick(parts, lambda i: row_from[i] // 2 == 2 * (y // 2) + 1)
+    tt[3] = pick(parts, lambda i: row_from[i] >= 4)
+    tt[4] = rows
+    tt[5] = pick(parts, lambda i: row_from[i] < 2 * y)
+    tt[6] = pick(parts, lambda i: jnp.logical_and(row_from[i] >= 4, row_from[i] < 2 * y))
+    tt[7] = jnp.zeros((H, N), F32)
+    off_ref[0] = jnp.zeros((H, N), F32)
+    off_ref[1] = jnp.where(b == 1, core0, 0.0)
+    off_ref[2] = pick(parts, lambda i: jnp.logical_and(row_from[i] >= 4 * (y // 2), row_from[i] < r))         if False else jnp.where(b == 1, core0, 0.0) + pick(
+            parts, lambda i: jnp.logical_and(row_from[i] // 2 == y - 1, yodd))
+    off3 = pick(parts, lambda i: row_from[i] < r)
+    off_ref[3] = off3
+
+    def z_tables():
+        for i in range(1, 8):
+            ztot(i).wait_recv()
+        zp = [tt[4]] + [zt[i] for i in range(1, 8)]
+        tt[8] = pick(zp, lambda i: jnp.logical_and(z_from[i] >= z - 1, z_from[i] <= z))
+        off_ref[4] = off_ref[3] + pick(zp, lambda i: jnp.logical_and(z_from[i] >= 2 * (z // 2), z_from[i] < z))
+        off_ref[5] = off_ref[3] + pick(zp, lambda i: jnp.logical_and(z_from[i] >= 4 * (z // 4), z_from[i] < z))
+
+    def tb(k, h):
+        return tt[k, pl.ds(mine + h, 1), :]
+
+    def merge(out, low, high, k, h):
+        out[...] = jnp.exp(tb(k, h)) * low[...] + high[...]
 
     def f1(h):
         x1(h).wait_recv()
 
         @pl.when(b == 0)
         def _():
-            merge(cbuf.at[h], s_ref.at[mine + h], b0_ref.at[mine + h], tot(b0_ref.at[mine + h]))
+            merge(cbuf.at[h], s_ref.at[mine + h], b0_ref.at[mine + h], 1, h)
 
         @pl.when(b == 1)
         def _():
-            merge(cbuf.at[h], b0_ref.at[mine + h], s_ref.at[mine + h], tot(s_ref.at[mine + h]))
+            merge(cbuf.at[h], b0_ref.at[mine + h], s_ref.at[mine + h], 1, h)
 
         y1(h).start()
 
@@ -229,12 +265,12 @@
 
         @pl.when(yodd)
         def _():
-            merge(mbuf.at[h], other, cbuf.at[h], tot(cbuf.at[h]))
+            merge(mbuf.at[h], other, cbuf.at[h], 2, h)
             x4(0, h).start()
 
         @pl.when(jnp.logical_not(yodd))
         def _():
-            merge(mbuf.at[h], cbuf.at[h], other, tot(other))
+            merge(mbuf.at[h], cbuf.at[h], other, 2, h)
 
         y2(h).start()
 
@@ -244,12 +280,12 @@
 
         @pl.when(yhi)
         def _():
-            merge(rbuf.at[h], other, mbuf.at[h], tot(mbuf.at[h]))
+            merge(rbuf.at[h], other, mbuf.at[h], 3, h)
             x4(1, h).start()
 
         @pl.when(jnp.logical_not(yhi))
         def _():
-            merge(rbuf.at[h], mbuf.at[h], other, tot(other))
+            merge(rbuf.at[h], mbuf.at[h], other, 3, h)
 
         @pl.when(jnp.logical_not(zb[0]))
         def _():
@@ -258,7 +294,7 @@
     def f4(h):
         zmsg(0, rbuf.at[h], h).wait_recv()
         x4(2, h).start()
-        merge(pbuf.at[h], bk_ref.at[2, mine + h], rbuf.at[h], tot(rbuf.at[h]))
+        merge(pbuf.at[h], bk_ref.at[2, mine + h], rbuf.at[h], 4, h)
 
         @pl.when(jnp.logical_not(zb[1]))
         def _():
@@ -276,7 +312,7 @@
 
         @pl.when(z == 3)
         def _():
-            merge(qbuf.at[h], here, pbuf.at[h], tot(pbuf.at[h]))
+            merge(qbuf.at[h], here, pbuf.at[h], 8, h)
             zmsg(2, qbuf.at[h], h).start()
 
     def f7(h):
@@ -289,55 +325,31 @@
 
         x4(4, h).start()
 
-    def base_tot(h):
-        own = tot(s_ref.at[mine + h])
-        other = tot(b0_ref.at[mine + h])
-        return jnp.where(b == 0, own, other)
-
-    def chip_grad(j, h, off):
-        e0 = jnp.exp(base_tot(h))
-        own = g_ref[j, mine + h]
-        other = rg[j, h]
-        low = jnp.where(b == 0, jnp.exp(off), e0 * jnp.exp(off))
-        high = jnp.where(b == 0, e0 * jnp.exp(off), jnp.exp(off))
-        return low * own + high * other
-
-    def row_off(h):
-        t1 = tot(bk_ref.at[0, mine + h])
-        t2 = tot(bk_ref.at[1, mine + h])
-        return jnp.where(yodd, t1, 0.0) + jnp.where(yhi, t2, 0.0)
+    def chip_grad(j, h, k):
+        x2(j, h).wait_recv()
+        e0 = jnp.exp(tb(0, h))
+        off = jnp.exp(tb(k, h))
+        low = jnp.where(b == 0, off, e0 * off)
+        high = jnp.where(b == 0, e0 * off, off)
+        return low * g_ref[j, mine + h] + high * rg[j, h]
 
     in_slot = [jnp.where(zb[1], 2, 1), jnp.where(zb[0], 2, 1), 2]
     d_slot = jnp.where(zb[0], jnp.where(zb[1], 2, 1), 0)
-
-    def back(h):
-        @pl.when(jnp.logical_not(zb[0]))
-        def _():
-            emsg(0, h).wait_recv()
-
-        @pl.when(zb[0] != zb[1])
-        def _():
-            emsg(1, h).wait_recv()
-
-        @pl.when(jnp.logical_and(z >= 3, z < 7))
-        def _():
-            emsg(2, h).wait_recv()
-
-        off = row_off(h)
-        ez = jnp.exp(tot(rbuf.at[h]))
-        for j in (2, 1, 0):
-            @pl.when(zb[j])
-            def _(j=j):
-                x2(3 + j, h).wait_recv()
-                fbuf[j, h] = ez * ebuf[in_slot[j], h] + chip_grad(3 + j, h, off)
-                emsg(j, h).start()
-
+    in_cond = [jnp.logical_not(zb[0]), zb[0] != zb[1], jnp.logical_and(z >= 3, z < 7)]
+
+    def e_send(j):
+        def go(h):
+            fbuf[j, h] = jnp.exp(tb(4, h)) * ebuf[in_slot[j], h] + chip_grad(3 + j, h, 5)
+            emsg(j, h).start()
+        return go
+
+    def e_wait(j):
+        return lambda h: emsg(j, h).wait_recv()
+
+    def a_send(h):
         @pl.when(yhi)
         def _():
-            x2(2, h).wait_recv()
-            e23 = jnp.exp(tot(mbuf.at[h]))
-            off2 = jnp.where(yodd, tot(bk_ref.at[0, mine + h]), 0.0)
-            abuf[h] = e23 * ebuf[d_slot, h] + chip_grad(2, h, off2)
+            abuf[h] = jnp.exp(tb(3, h)) * ebuf[d_slot, h] + chip_grad(2, h, 6)
 
         @pl.when(jnp.logical_not(yhi))
         def _():
@@ -347,14 +359,13 @@
 
     def ya(h):
         amsg(h).wait_recv()
-        e23 = jnp.where(yhi, 1.0, jnp.exp(tot(bk_ref.at[1, mine + h])))
+        e23 = jnp.where(yhi, 1.0, jnp.exp(tb(3, h)))
         yv = e23 * ebuf[d_slot, h] + ybuf[0, h]
         ybuf[2, h] = yv
 
         @pl.when(yodd)
         def _():
-            x2(1, h).wait_recv()
-            bbuf[h] = jnp.exp(tot(cbuf.at[h])) * yv + chip_grad(1, h, jnp.zeros((1, N), F32))
+            bbuf[h] = jnp.exp(tb(2, h)) * yv + chip_grad(1, h, 7)
 
         @pl.when(jnp.logical_not(yodd))
         def _():
@@ -364,24 +375,30 @@
 
     def yb(h):
         bmsg(h).wait_recv()
-        e1 = jnp.where(yodd, 1.0, jnp.exp(tot(bk_ref.at[0, mine + h])))
+        e1 = jnp.where(yodd, 1.0, jnp.exp(tb(2, h)))
         dc = e1 * ybuf[2, h] + ybuf[1, h]
 
         @pl.when(b == 0)
         def _():
             x2(0, h).wait_recv()
-            ds_ref[mine + h] = jnp.exp(tot(b0_ref.at[mine + h])) * dc + rg[0, h]
+            ds_ref[mine + h] = jnp.exp(tb(1, h)) * dc + rg[0, h]
             xbuf[h] = dc
 
         @pl.when(b == 1)
         def _():
             ds_ref[mine + h] = dc
-            xbuf[h] = jnp.exp(tot(s_ref.at[mine + h])) * dc + g_ref[0, mine + h]
+            xbuf[h] = jnp.exp(tb(1, h)) * dc + g_ref[0, mine + h]
 
         x5(h).start()
 
     d = GRAN
-    back0 = 2 * d
+    e5_lag = (7 - z) * d
+    low_half = z < 4
+    e4_lag = jnp.where(low_half, (7 - z) * d, HH + (7 - z) * d)
+    e3_lag = jnp.where(z == 7, 2 * HH, jnp.where(z == 5, HH + 2 * d, jnp.where(z == 3, HH + 4 * d, 6 * d)))
+    d_lag = jnp.where(z == 7, 0, jnp.where(z == 6, 2 * HH + d, jnp.where(z == 5, HH + 2 * d, jnp.where(
+        z == 4, HH + 3 * d, jnp.where(z == 3, 4 * d, jnp.where(z == 2, HH + 5 * d, jnp.where(z == 1, 6 * d, 7 * d)))))))
+    B0 = 1
 
     def tick(t, carry):
         def stage(fn, lag, cond=None):
@@ -394,18 +411,28 @@
             def _():
                 fn(h)
 
+        @pl.when(t == 3)
+        def _():
+            z_tables()
+
         stage(f1, 0)
+        stage(e_wait(2), B0 + e5_lag, in_cond[2])
+        stage(e_send(2), B0 + e5_lag, zb[2])
+        stage(e_wait(1), B0 + e4_lag, in_cond[1])
+        stage(e_send(1), B0 + e4_lag, zb[1])
         stage(f2, d)
         stage(f3, 2 * d)
-        stage(back, back0 + (7 - z) * d)
         stage(f4, 3 * d, zb[0])
         stage(f5, 4 * d + jnp.where(zb[0], d, 0), zb[1])
         stage(f7, 6 * d + (z - 4) * d, zb[2])
-        stage(ya, back0 + (8 - z) * d)
-        stage(yb, back0 + (9 - z) * d)
+        stage(e_send(0), B0 + e3_lag, zb[0])
+        stage(e_wait(0), B0 + d_lag, in_cond[0])
+        stage(a_send, B0 + d_lag)
+        stage(ya, B0 + d_lag + d)
+        stage(yb, B0 + d_lag + 2 * d)
         return carry
 
-    lax.fori_loop(0, HH + back0 + 9 * d, tick, 0)
+    lax.fori_loop(0, B0 + 3 * HH + 3 * d, tick, 0)
 
     def all_of(src, dst, send, recv):
         return copy(src, dst, send, recv, part)
@@ -414,59 +441,63 @@
     for j in range(5):
         def late(j=j):
             all_of(bk_ref.at[j, half], bk_ref.at[j, half], ssem.at[8 + j], rlate.at[j]).wait()
+            all_of(rg.at[j, half], rg.at[j, half], ssem.at[3 + j], rlate.at[j]).wait_send()
         pl.when(setbits[j + 1])(late)
-        def sent(j=j):
-            all_of(rg.at[j, half], rg.at[j, half], ssem.at[3 + j], rlate.at[j]).wait_send()
-        pl.when(setbits[j + 1])(sent)
+
+    def sent(k, buf):
+        all_of(buf.at[half], buf.at[half], ssem.at[k], rlate.at[5]).wait_send()
 
     @pl.when(b == 0)
     def _():
-        all_of(s_ref.at[half], s_ref.at[half], ssem.at[1], rlate.at[5]).wait_send()
+        sent(1, s_ref)
 
     @pl.when(b == 1)
     def _():
         all_of(s_ref.at[half], s_ref.at[half], ssem.at[1], rlate.at[5]).wait_recv()
-        all_of(rg.at[0, half], rg.at[0, half], ssem.at[2], rlate.at[5]).wait_send()
+        sent(2, cbuf)
 
     all_of(xbuf.at[half], xbuf.at[half], ssem.at[13], rlate.at[6]).wait()
-    all_of(s_ref.at[half], s_ref.at[half], ssem.at[0], rlate.at[5]).wait_send()
-    all_of(cbuf.at[half], cbuf.at[half], ssem.at[14], rlate.at[5]).wait_send()
-    all_of(mbuf.at[half], mbuf.at[half], ssem.at[15], rlate.at[5]).wait_send()
-    all_of(abuf.at[half], abuf.at[half], ssem.at[22], rlate.at[5]).wait_send()
-    all_of(bbuf.at[half], bbuf.at[half], ssem.at[23], rlate.at[5]).wait_send()
-    out_cond = [jnp.logical_not(zb[0]), zb[0] != zb[1], jnp.logical_and(z >= 3, z < 7)]
+    sent(0, cbuf)
+    for k in (14, 15, 22, 23):
+        sent(k, cbuf)
     for j in range(3):
         def zsent(j=j):
-            all_of(cbuf.at[half], cbuf.at[half], ssem.at[16 + j], rlate.at[5]).wait_send()
-        pl.when(out_cond[j])(zsent)
+            sent(16 + j, cbuf)
+        pl.when(in_cond[j])(zsent)
         def esent(j=j):
-            all_of(fbuf.at[j, half], fbuf.at[j, half], ssem.at[19 + j], rlate.at[5]).wait_send()
+            sent(19 + j, cbuf)
         pl.when(zb[j])(esent)
-
-
-def comm(s, big):
+    for i in range(1, 8):
+        rtot(i).wait_send()
+        ztot(i).wait_send()
+
+
+def comm(s, big, own):
     vm = pl.BlockSpec(memory_space=pltpu.VMEM)
-    st = lambda *lead: pltpu.VMEM(lead + (NR, N), F32)
     sg = lambda *lead: pltpu.VMEM(lead + (N, N), F32)
+    tv = lambda *lead: pltpu.VMEM(lead + (H, N), F32)
     dma = pltpu.SemaphoreType.DMA
     return pl.pallas_call(
         comm_kernel,
-        in_specs=[vm, vm],
-        out_specs=[vm, vm, vm],
-        out_shape=[jax.ShapeDtypeStruct((H, NR, N), F32),
-                   jax.ShapeDtypeStruct((XLEV - 1, H, NR, N), F32),
-                   jax.ShapeDtypeStruct((H, N, N), F32)],
-        scratch_shapes=[sg(6, HH), st(HH), st(HH), st(HH), st(HH), st(HH),
+        in_specs=[vm, vm, vm],
+        out_specs=[vm, vm, vm, vm],
+        out_shape=[jax.ShapeDtypeStruct((H, N, N), F32),
+                   jax.ShapeDtypeStruct((XLEV - 1, H, N, N), F32),
+                   jax.ShapeDtypeStruct((H, N, N), F32),
+                   jax.ShapeDtypeStruct((XLEV, H, N), F32)],
+        scratch_shapes=[sg(6, HH), sg(HH), sg(HH), sg(HH), sg(HH), sg(HH),
                         sg(3, HH), sg(3, HH), sg(HH), sg(HH), sg(3, HH), sg(HH),
+                        tv(9), tv(8), tv(8), tv(),
                         dma((24,)), dma((HH,)), dma((6, HH)), dma((HH,)), dma((HH,)),
-                        dma((3, HH)), dma((3, HH)), dma((HH,)), dma((HH,)), dma((7,))],
+                        dma((3, HH)), dma((3, HH)), dma((HH,)), dma((HH,)), dma((7,)),
+                        dma((8,)), dma((8,)), dma((8,)), dma((8,))],
         compiler_params=pltpu.CompilerParams(collective_id=0, has_side_effects=True,
                                              vmem_limit_bytes=62 * 1024 * 1024),
         name="states",
-    )(s, big)
-
-
-def final_kernel(q_ref, k_ref, v_ref, g_ref, gain_ref, decay_ref, b0_ref, bk_ref, ds_ref,
+    )(s, big, own)
+
+
+def final_kernel(q_ref, k_ref, v_ref, g_ref, gain_ref, decay_ref, b0_ref, bk_ref, ds_ref, off_ref,
                  o_ref, dq_ref, dk_ref, dv_ref, dgain_ref, rev_ref, tot_ref,
                  run_sc, tot_sc, row_sc, col_sc):
     h = pl.program_id(0)
@@ -489,15 +520,13 @@
     bits = [lax.rem(c // (1 << j), 2) == 1 for j in range(XLEV)]
     rows = []
     lifts = []
-    off = run
     buckets = []
     for j in range(XLEV):
         src = b0_ref.at[0] if j == 0 else bk_ref.at[j - 1, 0]
-        buckets.append(jnp.where(bits[j], src[0:N, :], 0.0))
-        lift = jnp.where(bits[j], jnp.exp(off), 0.0)
+        buckets.append(jnp.where(bits[j], src[...], 0.0))
+        lift = jnp.where(bits[j], jnp.exp(run + off_ref[j, pl.ds(h, 1), :]), 0.0)
         lifts.append(lift)
         rows.append(gain_ref[LVL_IN + j, pl.ds(h, 1), :] * lift)
-        off = off + jnp.where(bits[j], src[N:N + 1, :], 0.0)
     rows += [run, jnp.exp(tot - run)]
     cols = jnp.transpose(jnp.concatenate(rows + [jnp.zeros((N - 8, N), F32)], axis=0))
     run_col = cols[:, 6:7]
@@ -561,7 +590,7 @@
                                        preferred_element_type=F32)
 
 
-def final(q, k, v, g, gain, decay, b0, bk, ds):
+def final(q, k, v, g, gain, decay, b0, bk, ds, off):
     col = pl.BlockSpec((N, N), lambda h: (0, h))
     whole3 = pl.BlockSpec((LVL_IN + XLEV, H, N), lambda h: (0, 0, 0))
     whole2 = pl.BlockSpec((H, N), lambda h: (0, 0))
@@ -570,9 +599,10 @@
         final_kernel,
         grid=(H,),
         in_specs=[col, col, col, col, whole3, whole2,
-                  pl.BlockSpec((1, NR, N), lambda h: (h, 0, 0)),
-                  pl.BlockSpec((XLEV - 1, 1, NR, N), lambda h: (0, h, 0, 0)),
-                  pl.BlockSpec((1, N, N), lambda h: (h, 0, 0))],
+                  pl.BlockSpec((1, N, N), lambda h: (h, 0, 0)),
+                  pl.BlockSpec((XLEV - 1, 1, N, N), lambda h: (0, h, 0, 0)),
+                  pl.BlockSpec((1, N, N), lambda h: (h, 0, 0)),
+                  pl.BlockSpec((XLEV, H, N), lambda h: (0, 0, 0))],
         out_specs=[col, col, col, col, whole3, whole2, whole2],
         out_shape=[wide_out, wide_out, wide_out, wide_out,
                    jax.ShapeDtypeStruct((LVL_IN + XLEV, H, N), F32),
@@ -580,7 +610,7 @@
         scratch_shapes=[pltpu.VMEM((H, N), F32), pltpu.VMEM((H, N), F32),
                         pltpu.VMEM((H, N), F32), pltpu.VMEM((N, N), F32)],
         name="final",
-    )(q, k, v, g, gain, decay, b0, bk, ds)
+    )(q, k, v, g, gain, decay, b0, bk, ds, off)
 
 
 def suffix_kernel(rev_ref, tot_ref, out_ref, rowin, zin, sendbuf, ssem, rsem, zssem, zrsem):
@@ -641,9 +671,10 @@
 
 
 def per_device(queries, keys_in, value_input, level_gain, decay_log, out_grad):
-    s, big = front(queries, keys_in, value_input, out_grad, level_gain, decay_log)
-    b0, bk, ds = comm(s, big)
-    o, dq, dk, dv, dgain, rev, tot = final(queries, keys_in, value_input, out_grad, level_gain, decay_log, b0, bk, ds)
+    s, big, own = front(queries, keys_in, value_input, out_grad, level_gain, decay_log)
+    b0, bk, ds, off = comm(s, big, own)
+    o, dq, dk, dv, dgain, rev, tot = final(queries, keys_in, value_input, out_grad, level_gain, decay_log,
+                                           b0, bk, ds, off)
     return o, dq, dk, dv, dgain, suffix(rev, tot)
 
 

time: 137 us -> 126 us (0.920)
  Pallas kernels: 134 us -> 122 us
    pallas_call x1, Pallas kernels: 90.1 us -> 71.1 us  [comm(): pl.pallas_call(comm_kernel, in_specs=[vm, vm, vm], out_specs=[vm, vm, vm,...]
    pallas_call x1, Pallas kernels: 13.3 us -> 20.8 us  [suffix(): pl.pallas_call(suffix_kernel, in_specs=[vm, vm], out_specs=vm, out_shape=...]
where the time goes in v2:
time: 126 us; the launch traced here: 124 us
  Pallas kernels  122 us (97%)
  local copies, waits for them, and re-layouts  1.3 us (1%)
    pallas_call x1, Pallas kernels, comm(): pl.pallas_call(comm_kernel, in_specs=[vm, vm, vm], out_specs=[vm, vm, vm,...  71.1 us
    pallas_call x1, Pallas kernels, suffix(): pl.pallas_call(suffix_kernel, in_specs=[vm, vm], out_specs=vm, out_shape=...  20.8 us
    pallas_call x1, Pallas kernels, final(): pl.pallas_call(final_kernel, grid=(H,), in_specs=[col, col, col, col, who...  18 us
    pallas_call x1, Pallas kernels, front(): pl.pallas_call(front_kernel, grid=(H,), in_specs=[col, col, col, col, pl....  12.2 us

profile of v2, /device:TPU:1, one launch (start us, length us, event | category | flops | bytes accessed | tf_op | source)
XLA Modules:
  0.0 124.1 jit_solution(214961346049327640)
XLA Ops:
  0.6 12.2 %front.1 = (f32[16,128,128]{2,1,0:T(8,128)}, f32[6,16,128,128]{3,2,1,0:T(8,128)}, f32[16,128]{1,0:T(8,128)}) custom-call(bf16[128,2048]{1,0:T(8,128)(2,1)} %q_ref.3, bf16[128,2048]{1,0:T(8,128)(2,1)} %k_ref.3, bf16[128,2048]{1,0:T(8,128)(2,1)} %v_ref.3, bf16[128,2048]{1,0:T(8,128)(2,1)} %g_ref.3, f32[14,16,128]{2,1,0:T(8,128)} %gain_ref.3, f32[16,128]{1,0:T(8,128)} %decay_ref.3), custom_call_target="tpu_custom_call" | custom-call | tf_op jit(solution)/shard_map/front/pallas_call | solution.py:82
  12.9 71.1 %states.1 = (f32[16,128,128]{2,1,0:T(8,128)}, f32[5,16,128,128]{3,2,1,0:T(8,128)}, f32[16,128,128]{2,1,0:T(8,128)}, f32[6,16,128]{2,1,0:T(8,128)}) custom-call(f32[16,128,128]{2,1,0:T(8,128)} %get-tuple-element.20.s_ref, f32[6,16,128,128]{3,2,1,0:T(8,128)} %get-tuple-element.21.g_ref, f32[16,128]{1,0:T(8,128)} %get-tuple-element.22.own_ref), custom_call_target="tpu_custom_call" | custom-call | tf_op jit(solution)/shard_map/states/pallas_call | solution.py:480
  84.0 18.0 %final.1 = (bf16[128,2048]{1,0:T(8,128)(2,1)}, bf16[128,2048]{1,0:T(8,128)(2,1)}, bf16[128,2048]{1,0:T(8,128)(2,1)}, bf16[128,2048]{1,0:T(8,128)(2,1)}, f32[14,1...) custom-call(bf16[128,2048]{1,0:T(8,128)(2,1)} %q_ref.3, bf16[128,2048]{1,0:T(8,128)(2,1)} %k_ref.3, ...), custom_call_target="tpu_custom_call" | custom-call | tf_op jit(solution)/shard_map/final/pallas_call | solution.py:598
  102.0 20.8 %suffix.1 = f32[16,128]{1,0:T(8,128)} custom-call(f32[16,128]{1,0:T(8,128)} %get-tuple-element.32.rev_ref, f32[16,128]{1,0:T(8,128)} %get-tuple-element.33.tot_ref), custom_call_target="tpu_custom_call" | custom-call | tf_op jit(solution)/shard_map/suffix/pallas_call | solution.py:661
  122.8 1.3 %copy.13 = f32[16,128]{1,0:T(8,128)} copy(f32[16,128]{1,0:T(8,128)} %suffix.1) | data formatting | bytes 16384

commit v3 on v2

--- a/solution.py
+++ b/solution.py
@@ -13,7 +13,6 @@
 N = 128
 LVL_IN = 8
 XLEV = 6
-GRAN = 2
 
 NN = (((1,), (0,)), ((), ()))
 NT = (((1,), (1,)), ((), ()))
@@ -325,8 +324,9 @@
 
         x4(4, h).start()
 
-    def chip_grad(j, h, k):
-        x2(j, h).wait_recv()
+    def chip_grad(j, h, k, wait=True):
+        if wait:
+            x2(j, h).wait_recv()
         e0 = jnp.exp(tb(0, h))
         off = jnp.exp(tb(k, h))
         low = jnp.where(b == 0, off, e0 * off)
@@ -339,7 +339,13 @@
 
     def e_send(j):
         def go(h):
-            fbuf[j, h] = jnp.exp(tb(4, h)) * ebuf[in_slot[j], h] + chip_grad(3 + j, h, 5)
+            if j == 1:
+                @pl.when(z != 3)
+                def _():
+                    x2(4, h).wait_recv()
+            else:
+                x2(3 + j, h).wait_recv()
+            fbuf[j, h] = jnp.exp(tb(4, h)) * ebuf[in_slot[j], h] + chip_grad(3 + j, h, 5, False)
             emsg(j, h).start()
         return go
 
@@ -391,14 +397,40 @@
 
         x5(h).start()
 
-    d = GRAN
-    e5_lag = (7 - z) * d
-    low_half = z < 4
-    e4_lag = jnp.where(low_half, (7 - z) * d, HH + (7 - z) * d)
-    e3_lag = jnp.where(z == 7, 2 * HH, jnp.where(z == 5, HH + 2 * d, jnp.where(z == 3, HH + 4 * d, 6 * d)))
-    d_lag = jnp.where(z == 7, 0, jnp.where(z == 6, 2 * HH + d, jnp.where(z == 5, HH + 2 * d, jnp.where(
-        z == 4, HH + 3 * d, jnp.where(z == 3, 4 * d, jnp.where(z == 2, HH + 5 * d, jnp.where(z == 1, 6 * d, 7 * d)))))))
-    B0 = 1
+    def hop(n):
+        return (5 * n + 1) // 2
+
+    def by_z(vals):
+        out = jnp.int32(vals[7])
+        for i in range(7):
+            out = jnp.where(z == i, vals[i], out)
+        return out
+
+    far = 1000
+    e5_lag = by_z([far, far, far, hop(4), hop(3), hop(2), hop(1), far])
+    e4_in = by_z([far, hop(6), hop(5), far, far, HH + hop(2), HH + hop(1), far])
+    e4_out = by_z([far, far, hop(5), hop(4), far, far, HH + hop(1), far])
+    e3_out = by_z([far, hop(6), far, 0, far, HH + hop(2), far, far])
+    d_lag = by_z([hop(7), hop(6), hop(5), hop(4), HH + hop(3), HH + hop(2), 2 * HH + hop(1), 6])
+
+    def d_ready(h):
+        emsg(0, h).wait_recv()
+
+        @pl.when(z == 2)
+        def _():
+            ebuf[0, h] = ebuf[0, h] + ebuf[1, h]
+
+    def delta_send(h):
+        fbuf[0, h] = chip_grad(3, h, 5) - chip_grad(4, h, 5)
+        emsg(0, h).start()
+
+    @pl.when(z == 7)
+    def _():
+        each(e_send(2))
+        each(e_send(1))
+        each(e_send(0))
+
+    B0 = 2
 
     def tick(t, carry):
         def stage(fn, lag, cond=None):
@@ -411,28 +443,29 @@
             def _():
                 fn(h)
 
-        @pl.when(t == 3)
+        @pl.when(t == 6)
         def _():
             z_tables()
 
         stage(f1, 0)
-        stage(e_wait(2), B0 + e5_lag, in_cond[2])
-        stage(e_send(2), B0 + e5_lag, zb[2])
-        stage(e_wait(1), B0 + e4_lag, in_cond[1])
-        stage(e_send(1), B0 + e4_lag, zb[1])
-        stage(f2, d)
-        stage(f3, 2 * d)
-        stage(f4, 3 * d, zb[0])
-        stage(f5, 4 * d + jnp.where(zb[0], d, 0), zb[1])
-        stage(f7, 6 * d + (z - 4) * d, zb[2])
-        stage(e_send(0), B0 + e3_lag, zb[0])
-        stage(e_wait(0), B0 + d_lag, in_cond[0])
+        stage(e_wait(2), B0 + e5_lag)
+        stage(e_send(2), B0 + e5_lag, z > 3)
+        stage(e_wait(1), B0 + e4_in)
+        stage(e_send(1), B0 + e4_out)
+        stage(f2, hop(1))
+        stage(f3, hop(2))
+        stage(f4, hop(3), zb[0])
+        stage(f5, hop(4) + jnp.where(zb[0], hop(5) - hop(4), 0), zb[1])
+        stage(f7, by_z([far, far, far, far, hop(6), hop(7), hop(8), hop(9)]))
+        stage(delta_send, B0 + e3_out, z == 3)
+        stage(e_send(0), B0 + e3_out, z != 3)
+        stage(d_ready, B0 + d_lag, in_cond[0])
         stage(a_send, B0 + d_lag)
-        stage(ya, B0 + d_lag + d)
-        stage(yb, B0 + d_lag + 2 * d)
+        stage(ya, B0 + d_lag + hop(1))
+        stage(yb, B0 + d_lag + hop(2))
         return carry
 
-    lax.fori_loop(0, B0 + 3 * HH + 3 * d, tick, 0)
+    lax.fori_loop(0, B0 + 3 * HH + hop(3), tick, 0)
 
     def all_of(src, dst, send, recv):
         return copy(src, dst, send, recv, part)

time: 126 us -> 120 us (0.952)
  Pallas kernels: 122 us -> 117 us
    pallas_call x1, Pallas kernels: 20.8 us -> 15.9 us  [suffix(): pl.pallas_call(suffix_kernel, in_specs=[vm, vm], out_specs=vm, out_shape=...]
where the time goes in v3:
time: 120 us; the launch traced here: 119 us
  Pallas kernels  117 us (98%)
  local copies, waits for them, and re-layouts  1.3 us (1%)
    pallas_call x1, Pallas kernels, comm(): pl.pallas_call(comm_kernel, in_specs=[vm, vm, vm], out_specs=[vm, vm, vm,...  70.5 us
    pallas_call x1, Pallas kernels, final(): pl.pallas_call(final_kernel, grid=(H,), in_specs=[col, col, col, col, who...  18 us
    pallas_call x1, Pallas kernels, suffix(): pl.pallas_call(suffix_kernel, in_specs=[vm, vm], out_specs=vm, out_shape=...  15.9 us
    pallas_call x1, Pallas kernels, front(): pl.pallas_call(front_kernel, grid=(H,), in_specs=[col, col, col, col, pl....  12.2 us

profile of v3, /device:TPU:1, one launch (start us, length us, event | category | flops | bytes accessed | tf_op | source)
XLA Modules:
  0.0 118.6 jit_solution(3622942242776431780)
XLA Ops:
  0.6 12.2 %front.1 = (f32[16,128,128]{2,1,0:T(8,128)}, f32[6,16,128,128]{3,2,1,0:T(8,128)}, f32[16,128]{1,0:T(8,128)}) custom-call(bf16[128,2048]{1,0:T(8,128)(2,1)} %q_ref.3, bf16[128,2048]{1,0:T(8,128)(2,1)} %k_ref.3, bf16[128,2048]{1,0:T(8,128)(2,1)} %v_ref.3, bf16[128,2048]{1,0:T(8,128)(2,1)} %g_ref.3, f32[14,16,128]{2,1,0:T(8,128)} %gain_ref.3, f32[16,128]{1,0:T(8,128)} %decay_ref.3), custom_call_target="tpu_custom_call" | custom-call | tf_op jit(solution)/shard_map/front/pallas_call | solution.py:81
  12.9 70.5 %states.1 = (f32[16,128,128]{2,1,0:T(8,128)}, f32[5,16,128,128]{3,2,1,0:T(8,128)}, f32[16,128,128]{2,1,0:T(8,128)}, f32[6,16,128]{2,1,0:T(8,128)}) custom-call(f32[16,128,128]{2,1,0:T(8,128)} %get-tuple-element.20.s_ref, f32[6,16,128,128]{3,2,1,0:T(8,128)} %get-tuple-element.21.g_ref, f32[16,128]{1,0:T(8,128)} %get-tuple-element.22.own_ref), custom_call_target="tpu_custom_call" | custom-call | tf_op jit(solution)/shard_map/states/pallas_call | solution.py:513
  83.4 18.0 %final.1 = (bf16[128,2048]{1,0:T(8,128)(2,1)}, bf16[128,2048]{1,0:T(8,128)(2,1)}, bf16[128,2048]{1,0:T(8,128)(2,1)}, bf16[128,2048]{1,0:T(8,128)(2,1)}, f32[14,1...) custom-call(bf16[128,2048]{1,0:T(8,128)(2,1)} %q_ref.3, bf16[128,2048]{1,0:T(8,128)(2,1)} %k_ref.3, ...), custom_call_target="tpu_custom_call" | custom-call | tf_op jit(solution)/shard_map/final/pallas_call | solution.py:631
  101.4 15.9 %suffix.1 = f32[16,128]{1,0:T(8,128)} custom-call(f32[16,128]{1,0:T(8,128)} %get-tuple-element.32.rev_ref, f32[16,128]{1,0:T(8,128)} %get-tuple-element.33.tot_ref), custom_call_target="tpu_custom_call" | custom-call | tf_op jit(solution)/shard_map/suffix/pallas_call | solution.py:694
  117.3 1.3 %copy.13 = f32[16,128]{1,0:T(8,128)} copy(f32[16,128]{1,0:T(8,128)} %suffix.1) | data formatting | bytes 16384

commit v4 on v3

v4 whole, which is shorter than its diff:
```python
import jax
import jax.numpy as jnp
from jax import lax
from jax.experimental import pallas as pl
from jax.experimental.pallas import tpu as pltpu
from jax.sharding import PartitionSpec as P

MESH = pl.DeviceIdType.MESH
F32 = jnp.float32
BF16 = jnp.bfloat16
H = 16
HH = 8
N = 128
LVL_IN = 8
XLEV = 6

NN = (((1,), (0,)), ((), ()))
NT = (((1,), (1,)), ((), ()))


def mm(a, b, dims=NN):
    return lax.dot_general(a, b, dims, preferred_element_type=F32)


def split(x):
    hi = x.astype(BF16)
    lo = (x - hi.astype(F32)).astype(BF16)
    return hi, lo


def wide(x):
    hi, lo = split(x)
    return jnp.concatenate([hi, lo], axis=1)


def tall(x):
    hi, lo = split(x)
    return jnp.concatenate([hi, lo], axis=0)


def flip(x):
    return jnp.transpose(x.astype(F32)).astype(BF16)


def running_sums(decay):
    r = lax.broadcasted_iota(jnp.int32, (N, N), 0)
    t = lax.broadcasted_iota(jnp.int32, (N, N), 1)
    upper = (r <= t).astype(F32)
    run = lax.dot_general(decay, upper, NN, precision=lax.Precision.HIGHEST, preferred_element_type=F32)
    tot = lax.dot_general(decay, jnp.ones((N, N), F32), NN, precision=lax.Precision.HIGHEST, preferred_element_type=F32)
    return run, tot


def coords():
    c = lax.axis_index("ctx")
    return c, lax.rem(c, 2), lax.rem(c // 2, 4), c // 8


def pick(parts, cond):
    acc = jnp.zeros((H, N), F32)
    for i in range(8):
        acc = acc + jnp.where(cond(i), parts[i], 0.0)
    return acc


def fused_kernel(q_ref, k_ref, v_ref, g_ref, gain_ref, decay_ref,
                 o_ref, dq_ref, dk_ref, dv_ref, dgain_ref, ddecay_ref,
                 st, g_st, b0, bk, ds, oacc, dqacc, dkacc, dvacc, qt_sc, kt_sc, gt_sc,
                 rg, cbuf, mbuf, rbuf, pbuf, qbuf, ebuf, fbuf, abuf, bbuf, ybuf, xbuf,
                 tt, rowt, zt, rowf, zf, off, rsum, own, run_sc, row_sc, flux, zflux_sum, col_sc,
                 ssem, rx1, rx1b, rx2, rx4, rx5, ry1, ry2, rz, re, ra, rb,
                 trs, trr, tzs, tzr, frs, frr, fzs, fzr):
    seq = lax.axis_index("seq")
    c, b, y, z = coords()
    r = lax.rem(c, 8)
    mine = b * HH
    theirs = (1 - b) * HH
    part = c + 1 - 2 * b
    yn = c + 2 - 4 * lax.rem(y, 2)
    ym = c + 2 * (3 - 2 * y)
    up = c + 8
    dn = c - 8
    yodd = lax.rem(y, 2) == 1
    yhi = y >= 2
    zb = [lax.rem(z, 2) == 1, lax.rem(z // 2, 2) == 1, z >= 4]
    row_peer = [z * 8 + lax.rem(r + i, 8) for i in range(8)]
    z_peer = [lax.rem(z + i, 8) * 8 + r for i in range(8)]
    row_from = [lax.rem(r - i + 8, 8) for i in range(8)]
    z_from = [lax.rem(z - i + 8, 8) for i in range(8)]

    barrier = pltpu.get_barrier_semaphore()
    for i in range(1, 8):
        pl.semaphore_signal(barrier, inc=1, device_id=(seq, row_peer[i]), device_id_type=MESH)
        pl.semaphore_signal(barrier, inc=1, device_id=(seq, z_peer[i]), device_id_type=MESH)
    run, tot = running_sums(decay_ref[...])
    run_sc[...] = run
    own[...] = tot
    dgain_ref[...] = jnp.zeros((LVL_IN + XLEV, H, N), F32)
    pl.semaphore_wait(barrier, 14)

    def copy(src, dst, send, recv, who):
        return pltpu.make_async_remote_copy(src_ref=src, dst_ref=dst, send_sem=send, recv_sem=recv,
                                            device_id=(seq, who), device_id_type=MESH)

    def x1(h):
        return copy(st.at[theirs + h], b0.at[theirs + h], ssem.at[0], rx1.at[h], part)

    def x1b(h):
        return copy(st.at[h], b0.at[h], ssem.at[1], rx1b.at[h], part)

    def x2(j, h):
        return copy(g_st.at[j, theirs + h], rg.at[j, h], ssem.at[2 + j], rx2.at[j, h], part)

    def x4(j, h):
        return copy(bk.at[j, mine + h], bk.at[j, mine + h], ssem.at[8 + j], rx4.at[j, h], part)

    def x5(h):
        return copy(xbuf.at[h], ds.at[mine + h], ssem.at[13], rx5.at[h], part)

    def y1(h):
        return copy(cbuf.at[h], bk.at[0, mine + h], ssem.at[14], ry1.at[h], yn)

    def y2(h):
        return copy(mbuf.at[h], bk.at[1, mine + h], ssem.at[15], ry2.at[h], ym)

    def zmsg(j, src, h):
        return copy(src, bk.at[2 + j, mine + h], ssem.at[16 + j], rz.at[j, h], up)

    def emsg(j, h):
        return copy(fbuf.at[j, h], ebuf.at[j, h], ssem.at[19 + j], re.at[j, h], dn)

    def amsg(h):
        return copy(abuf.at[h], ybuf.at[0, h], ssem.at[22], ra.at[h], ym)

    def bmsg(h):
        return copy(bbuf.at[h], ybuf.at[1, h], ssem.at[23], rb.at[h], yn)

    def rtot(i):
        return copy(own, rowt.at[i], trs.at[i], trr.at[i], row_peer[i])

    def ztot(i):
        return copy(rsum, zt.at[i], tzs.at[i], tzr.at[i], z_peer[i])

    def rflux(i):
        return copy(flux, rowf.at[i], frs.at[i], frr.at[i], row_peer[i])

    def zflux(i):
        return copy(zflux_sum, zf.at[i], fzs.at[i], fzr.at[i], z_peer[i])

    setbits = [None, yodd, yhi, zb[0], zb[1], zb[2]]

    def each(fn):
        def body(h, carry):
            fn(h)
            return carry
        lax.fori_loop(0, HH, body, 0)

    for i in range(1, 8):
        rtot(i).start()

    def cols(h):
        return pl.ds(pl.multiple_of(h * N, N), N)

    def row(ref, h):
        return ref[pl.ds(h, 1), :]

    def make_state(h):
        kt = jnp.transpose(k_ref[:, cols(h)].astype(F32))
        kt_sc[h] = kt.astype(BF16)
        v = v_ref[:, cols(h)]
        st[h] = mm(wide(kt * jnp.exp(row(own, h) - row(run_sc, h))), jnp.concatenate([v, v], axis=0))

    def make_turned(h):
        qt_sc[h] = flip(q_ref[:, cols(h)])
        gt_sc[h] = flip(g_ref[:, cols(h)])

    def make_grad(j, h):
        g = g_ref[:, cols(h)]
        scale = gain_ref[LVL_IN + j, pl.ds(h, 1), :] * jnp.exp(row(run_sc, h))
        g_st[j, h] = mm(wide(qt_sc[h].astype(F32) * scale), jnp.concatenate([g, g], axis=0))

    def state_theirs(h):
        make_state(theirs + h)
        x1(h).start()

    def state_mine(h):
        make_state(mine + h)

        @pl.when(b == 0)
        def _():
            x1b(h).start()

    each(state_theirs)
    each(state_mine)

    @pl.when(z == 7)
    def _():
        def zero(h):
            ebuf[2, h] = jnp.zeros((N, N), F32)
        each(zero)

    for i in range(1, 8):
        rtot(i).wait_recv()
    parts = [own[...]] + [rowt[i] for i in range(1, 8)]
    rows = pick(parts, lambda i: row_from[i] >= 0)
    rsum[...] = rows
    for i in range(1, 8):
        ztot(i).start()
    core0 = pick(parts, lambda i: row_from[i] == 2 * y)
    core1 = pick(parts, lambda i: row_from[i] == 2 * y + 1)
    tt[0] = core0
    tt[1] = core1
    tt[2] = pick(parts, lambda i: row_from[i] // 2 == 2 * (y // 2) + 1)
    tt[3] = pick(parts, lambda i: row_from[i] >= 4)
    tt[4] = rows
    tt[5] = pick(parts, lambda i: row_from[i] < 2 * y)
    tt[6] = pick(parts, lambda i: jnp.logical_and(row_from[i] >= 4, row_from[i] < 2 * y))
    tt[7] = jnp.zeros((H, N), F32)
    off[0] = jnp.zeros((H, N), F32)
    off[1] = jnp.where(b == 1, core0, 0.0)
    off[2] = pick(parts, lambda i: jnp.logical_and(row_from[i] >= 4 * (y // 2), row_from[i] < r))         if False else jnp.where(b == 1, core0, 0.0) + pick(
            parts, lambda i: jnp.logical_and(row_from[i] // 2 == y - 1, yodd))
    off3 = pick(parts, lambda i: row_from[i] < r)
    off[3] = off3

    def z_tables():
        for i in range(1, 8):
            ztot(i).wait_recv()
        zp = [tt[4]] + [zt[i] for i in range(1, 8)]
        tt[8] = pick(zp, lambda i: jnp.logical_and(z_from[i] >= z - 1, z_from[i] <= z))
        off[4] = off[3] + pick(zp, lambda i: jnp.logical_and(z_from[i] >= 2 * (z // 2), z_from[i] < z))
        off[5] = off[3] + pick(zp, lambda i: jnp.logical_and(z_from[i] >= 4 * (z // 4), z_from[i] < z))

    def tb(k, h):
        return tt[k, pl.ds(mine + h, 1), :]

    def merge(out, low, high, k, h):
        out[...] = jnp.exp(tb(k, h)) * low[...] + high[...]

    def f1(h):
        x1(h).wait_recv()

        @pl.when(b == 0)
        def _():
            merge(cbuf.at[h], st.at[mine + h], b0.at[mine + h], 1, h)

        @pl.when(b == 1)
        def _():
            merge(cbuf.at[h], b0.at[mine + h], st.at[mine + h], 1, h)

        y1(h).start()

    def f2(h):
        y1(h).wait_recv()
        other = bk.at[0, mine + h]

        @pl.when(yodd)
        def _():
            merge(mbuf.at[h], other, cbuf.at[h], 2, h)
            x4(0, h).start()

        @pl.when(jnp.logical_not(yodd))
        def _():
            merge(mbuf.at[h], cbuf.at[h], other, 2, h)

        y2(h).start()

    def f3(h):
        y2(h).wait_recv()
        other = bk.at[1, mine + h]

        @pl.when(yhi)
        def _():
            merge(rbuf.at[h], other, mbuf.at[h], 3, h)
            x4(1, h).start()

        @pl.when(jnp.logical_not(yhi))
        def _():
            merge(rbuf.at[h], mbuf.at[h], other, 3, h)

        @pl.when(jnp.logical_not(zb[0]))
        def _():
            zmsg(0, rbuf.at[h], h).start()

    def f4(h):
        zmsg(0, rbuf.at[h], h).wait_recv()
        x4(2, h).start()
        merge(pbuf.at[h], bk.at[2, mine + h], rbuf.at[h], 4, h)

        @pl.when(jnp.logical_not(zb[1]))
        def _():
            zmsg(1, pbuf.at[h], h).start()

    def f5(h):
        here = bk.at[3, mine + h]
        zmsg(1, here, h).wait_recv()

        @pl.when(jnp.logical_not(zb[0]))
        def _():
            zmsg(1, here, h).start()

        x4(3, h).start()

        @pl.when(z == 3)
        def _():
            merge(qbuf.at[h], here, pbuf.at[h], 8, h)
            zmsg(2, qbuf.at[h], h).start()

    def f7(h):
        here = bk.at[4, mine + h]
        zmsg(2, here, h).wait_recv()

        @pl.when(z < 7)
        def _():
            zmsg(2, here, h).start()

        x4(4, h).start()

    def chip_grad(j, h, k, wait=True):
        if wait:
            x2(j, h).wait_recv()
        e0 = jnp.exp(tb(0, h))
        off = jnp.exp(tb(k, h))
        low = jnp.where(b == 0, off, e0 * off)
        high = jnp.where(b == 0, e0 * off, off)
        return low * g_st[j, mine + h] + high * rg[j, h]

    in_slot = [jnp.where(zb[1], 2, 1), jnp.where(zb[0], 2, 1), 2]
    d_slot = jnp.where(zb[0], jnp.where(zb[1], 2, 1), 0)
    in_cond = [jnp.logical_not(zb[0]), zb[0] != zb[1], jnp.logical_and(z >= 3, z < 7)]

    def e_send(j):
        def go(h):
            if j == 1:
                @pl.when(z != 3)
                def _():
                    x2(4, h).wait_recv()
            else:
                x2(3 + j, h).wait_recv()
            fbuf[j, h] = jnp.exp(tb(4, h)) * ebuf[in_slot[j], h] + chip_grad(3 + j, h, 5, False)
            emsg(j, h).start()
        return go

    def e_wait(j):
        return lambda h: emsg(j, h).wait_recv()

    def a_send(h):
        @pl.when(yhi)
        def _():
            abuf[h] = jnp.exp(tb(3, h)) * ebuf[d_slot, h] + chip_grad(2, h, 6)

        @pl.when(jnp.logical_not(yhi))
        def _():
            abuf[h] = ebuf[d_slot, h]

        amsg(h).start()

    def ya(h):
        amsg(h).wait_recv()
        e23 = jnp.where(yhi, 1.0, jnp.exp(tb(3, h)))
        yv = e23 * ebuf[d_slot, h] + ybuf[0, h]
        ybuf[2, h] = yv

        @pl.when(yodd)
        def _():
            bbuf[h] = jnp.exp(tb(2, h)) * yv + chip_grad(1, h, 7)

        @pl.when(jnp.logical_not(yodd))
        def _():
            bbuf[h] = yv

        bmsg(h).start()

    def yb(h):
        bmsg(h).wait_recv()
        e1 = jnp.where(yodd, 1.0, jnp.exp(tb(2, h)))
        dc = e1 * ybuf[2, h] + ybuf[1, h]

        @pl.when(b == 0)
        def _():
            x2(0, h).wait_recv()
            ds[mine + h] = jnp.exp(tb(1, h)) * dc + rg[0, h]
            xbuf[h] = dc

        @pl.when(b == 1)
        def _():
            ds[mine + h] = dc
            xbuf[h] = jnp.exp(tb(1, h)) * dc + g_st[0, mine + h]

        x5(h).start()

    def intra(h):
        run_h = row(run_sc, h)
        run_col = jnp.transpose(jnp.broadcast_to(run_h, (N, N)))
        q, k, v, g = (x[:, cols(h)] for x in (q_ref, k_ref, v_ref, g_ref))
        qt, gt, kt = qt_sc[h], gt_sc[h], kt_sc[h]
        vt = flip(v)
        s_i = lax.broadcasted_iota(jnp.int32, (N, N), 0)
        t_i = lax.broadcasted_iota(jnp.int32, (N, N), 1)
        causal = s_i <= t_i
        mixing = jnp.bitwise_xor(s_i, t_i)
        fade = jnp.where(causal, jnp.exp(jnp.where(causal, run_h - run_col, 0.0)), 0.0)
        weight = jnp.broadcast_to(gain_ref[0, pl.ds(h, 1), :], (N, N))
        for lev in range(1, LVL_IN):
            weight = jnp.where(mixing >= (1 << (lev - 1)), gain_ref[lev, pl.ds(h, 1), :], weight)
        sc = mm(k, qt)
        gv = mm(v, gt)
        wd = weight * fade
        wt = sc * wd
        xt = gv * wd
        pair = sc * gv * fade
        above = [jnp.sum(pair, axis=0, keepdims=True)]
        for lev in range(1, LVL_IN):
            above.append(jnp.sum(jnp.where(mixing >= (1 << (lev - 1)), pair, 0.0), axis=0, keepdims=True))
        above.append(jnp.zeros((1, N), F32))
        for lev in range(LVL_IN):
            dgain_ref[lev, pl.ds(h, 1), :] = above[lev] - above[lev + 1]
        oacc[h] = jnp.transpose(mm(jnp.concatenate([vt, vt], axis=1), tall(wt)))
        dqt = mm(jnp.concatenate([kt, kt], axis=1), tall(xt))
        dqacc[h] = dqt
        row_sc[pl.ds(h, 1), :] = jnp.sum(dqt * qt.astype(F32), axis=0, keepdims=True)
        dvacc[h] = mm(wide(wt), jnp.concatenate([g, g], axis=0))
        dkacc[h] = mm(wide(xt), jnp.concatenate([q, q], axis=0))

    def level(j, h):
        lift = jnp.exp(row(run_sc, h) + off[j, pl.ds(h, 1), :])
        scale = gain_ref[LVL_IN + j, pl.ds(h, 1), :] * lift
        q = q_ref[:, cols(h)]
        gt = gt_sc[h]
        m_hi, m_lo = split(b0[h] if j == 0 else bk[j - 1, h])
        part_o = mm(jnp.concatenate([q, q], axis=1), jnp.concatenate([m_hi, m_lo], axis=0))
        oacc[h] = oacc[h] + jnp.transpose(jnp.broadcast_to(scale, (N, N))) * part_o
        dt = mm(jnp.concatenate([m_hi, m_lo], axis=1), jnp.concatenate([gt, gt], axis=0))
        dqacc[h] = dqacc[h] + scale * dt
        sums = jnp.sum(dt * qt_sc[h].astype(F32), axis=0, keepdims=True)
        dgain_ref[LVL_IN + j, pl.ds(h, 1), :] = lift * sums
        row_sc[pl.ds(h, 1), :] = row_sc[pl.ds(h, 1), :] + scale * sums

    def level_own(j):
        return lambda h: level(j, mine + h)

    def level_other(j):
        def go(h):
            if j == 0:
                x1b(h).wait_recv()
            else:
                copy(bk.at[j - 1, theirs + h], bk.at[j - 1, theirs + h], ssem.at[7 + j], rx4.at[j - 1, h],
                     part).wait_recv()
            level(j, theirs + h)
        return go

    def tail_terms(h):
        tail = jnp.transpose(jnp.broadcast_to(jnp.exp(row(own, h) - row(run_sc, h)), (N, N)))
        k, v = k_ref[:, cols(h)], v_ref[:, cols(h)]
        d_hi, d_lo = split(ds[h])
        dv = dvacc[h] + tail * mm(jnp.concatenate([k, k], axis=1), jnp.concatenate([d_hi, d_lo], axis=0))
        dk = dkacc[h] + tail * mm(jnp.concatenate([v, v], axis=1), jnp.concatenate([d_hi, d_lo], axis=1), NT)
        dk_ref[:, cols(h)] = dk.astype(BF16)
        dv_ref[:, cols(h)] = dv.astype(BF16)
        t_i = lax.broadcasted_iota(jnp.int32, (N, N), 1)
        col_sc[...] = jnp.where(t_i == h, jnp.sum(v.astype(F32) * dv, axis=1, keepdims=True), col_sc[...])

    def tail_own(h):
        tail_terms(mine + h)

    def tail_other(h):
        copy(ds.at[theirs + h], ds.at[theirs + h], ssem.at[13], rx5.at[h], part).wait_recv()
        tail_terms(theirs + h)

    def grads_early(i):
        h = lax.rem(theirs + i, H)
        make_turned(h)

        for j in (5, 4, 3):
            @pl.when(setbits[j])
            def _(j=j):
                make_grad(j, h)

                @pl.when(i < HH)
                def _():
                    x2(j, i).start()

    def grads_late(i):
        h = lax.rem(theirs + i, H)
        for j in (2, 1, 0):
            @pl.when(b == 1 if j == 0 else setbits[j])
            def _(j=j):
                make_grad(j, h)

                @pl.when(i < HH)
                def _():
                    x2(j, i).start()

    def hop(n):
        return (5 * n + 1) // 2

    def by_z(vals):
        out = jnp.int32(vals[7])
        for i in range(7):
            out = jnp.where(z == i, vals[i], out)
        return out

    far = 1000
    e5_lag = by_z([far, far, far, hop(4), hop(3), hop(2), hop(1), far])
    e4_in = by_z([far, hop(6), hop(5), far, far, HH + hop(2), HH + hop(1), far])
    e4_out = by_z([far, far, hop(5), hop(4), far, far, HH + hop(1), far])
    e3_out = by_z([far, hop(6), far, 0, far, HH + hop(2), far, far])
    d_lag = by_z([hop(7), hop(6), hop(5), hop(4), HH + hop(3), HH + hop(2), 2 * HH + hop(1), 8])
    f7_lag = by_z([far, far, far, far, hop(6), hop(7), hop(8), hop(9)])

    def d_ready(h):
        emsg(0, h).wait_recv()

        @pl.when(z == 2)
        def _():
            ebuf[0, h] = ebuf[0, h] + ebuf[1, h]

    def delta_send(h):
        fbuf[0, h] = chip_grad(3, h, 5) - chip_grad(4, h, 5)
        emsg(0, h).start()

    def early(i, carry):
        grads_early(i)
        return carry

    col_sc[...] = jnp.zeros((N, N), F32)
    each(f1)
    lax.fori_loop(0, H, early, 0)

    @pl.when(z == 7)
    def _():
        each(e_send(2))
        each(e_send(1))
        each(e_send(0))

    B0 = 2

    def tick(t, carry):
        def stage(fn, lag, cond=None, count=HH):
            h = t - lag
            ok = jnp.logical_and(h >= 0, h < count)
            if cond is not None:
                ok = jnp.logical_and(ok, cond)

            @pl.when(ok)
            def _():
                fn(h)

        @pl.when(t == 5)
        def _():
            z_tables()

        stage(e_wait(2), B0 + e5_lag)
        stage(e_send(2), B0 + e5_lag, z > 3)
        stage(e_wait(1), B0 + e4_in)
        stage(e_send(1), B0 + e4_out)
        stage(f2, 0)
        stage(f3, hop(2) - hop(1))
        stage(f4, hop(3) - hop(1), zb[0])
        stage(f5, hop(4) - hop(1) + jnp.where(zb[0], hop(5) - hop(4), 0), zb[1])
        stage(f7, f7_lag - hop(1))
        stage(delta_send, B0 + e3_out, z == 3)
        stage(e_send(0), B0 + e3_out, z != 3)
        stage(grads_late, 0, count=H)
        stage(d_ready, B0 + d_lag, in_cond[0])
        stage(a_send, B0 + d_lag)
        stage(ya, B0 + d_lag + hop(1))
        stage(yb, B0 + d_lag + hop(2))
        stage(tail_own, B0 + d_lag + hop(2) + 1)
        stage(tail_other, B0 + d_lag + hop(2) + 2)
        stage(lambda i: intra(lax.rem(mine + i, H)), 0, count=H)
        stage(level_own(0), 2, b == 1)
        stage(level_own(1), 3, setbits[1])
        stage(level_own(2), 6, setbits[2])
        stage(level_own(3), 7, setbits[3])
        stage(level_own(4), 12, setbits[4])
        stage(level_own(5), f7_lag - hop(1) + 1, setbits[5])
        stage(level_other(0), 20, b == 1)
        stage(level_other(1), 15, setbits[1])
        stage(level_other(2), 17, setbits[2])
        stage(level_other(3), 13, setbits[3])
        stage(level_other(4), 14, setbits[4])
        stage(level_other(5), f7_lag - hop(1) + 2, setbits[5])
        return carry

    lax.fori_loop(0, B0 + 3 * HH + hop(4), tick, 0)

    da = row_sc[...] - jnp.transpose(col_sc[...])[0:H, :]
    s_i = lax.broadcasted_iota(jnp.int32, (N, N), 0)
    t_i = lax.broadcasted_iota(jnp.int32, (N, N), 1)
    flux[...] = lax.dot_general(da, jnp.ones((N, N), F32), NN, precision=lax.Precision.HIGHEST,
                                preferred_element_type=F32)
    for i in range(1, 8):
        rflux(i).start()

    def put_out(h):
        o_ref[:, cols(h)] = oacc[h].astype(BF16)
        dq_ref[:, cols(h)] = jnp.transpose(dqacc[h]).astype(BF16)

    def put(h, carry):
        put_out(h)
        return carry

    lax.fori_loop(0, HH, put, 0)
    total = flux[...]
    after = lax.dot_general(da, (s_i >= t_i).astype(F32), NN, precision=lax.Precision.HIGHEST,
                            preferred_element_type=F32)
    for i in range(1, 8):
        rflux(i).wait_recv()
        val = rowf[i]
        total = total + val
        after = after + jnp.where(row_from[i] > r, val, 0.0)
    zflux_sum[...] = total
    for i in range(1, 8):
        zflux(i).start()
    lax.fori_loop(HH, H, put, 0)
    for i in range(1, 8):
        zflux(i).wait_recv()
        after = after + jnp.where(z_from[i] > z, zf[i], 0.0)
    ddecay_ref[...] = after

    def all_of(src, dst, send, recv):
        return copy(src, dst, send, recv, part)

    half = pl.ds(0, HH)

    def sent(k, buf):
        all_of(buf.at[half], buf.at[half], ssem.at[k], rx1.at[0]).wait_send()

    for j in range(5):
        def late(j=j):
            sent(8 + j, cbuf)
            sent(3 + j, cbuf)
        pl.when(setbits[j + 1])(late)

    @pl.when(b == 0)
    def _():
        sent(1, cbuf)

    @pl.when(b == 1)
    def _():
        sent(2, cbuf)

    sent(0, cbuf)
    for k in (13, 14, 15, 22, 23):
        sent(k, cbuf)
    for j in range(3):
        def zsent(j=j):
            sent(16 + j, cbuf)
        pl.when(in_cond[j])(zsent)
        def esent(j=j):
            sent(19 + j, cbuf)
        pl.when(zb[j])(esent)
    for i in range(1, 8):
        rtot(i).wait_send()
        ztot(i).wait_send()
        rflux(i).wait_send()
        zflux(i).wait_send()


def fused(q, k, v, g, gain, decay):
    vm = pl.BlockSpec(memory_space=pltpu.VMEM)
    sg = lambda *lead: pltpu.VMEM(lead + (N, N), F32)
    sh = lambda *lead: pltpu.VMEM(lead + (N, N), BF16)
    tv = lambda *lead: pltpu.VMEM(lead + (H, N), F32)
    dma = pltpu.SemaphoreType.DMA
    wide_out = jax.ShapeDtypeStruct((N, H * N), BF16)
    return pl.pallas_call(
        fused_kernel,
        in_specs=[vm] * 6,
        out_specs=[vm] * 6,
        out_shape=[wide_out, wide_out, wide_out, wide_out,
                   jax.ShapeDtypeStruct((LVL_IN + XLEV, H, N), F32),
                   jax.ShapeDtypeStruct((H, N), F32)],
        scratch_shapes=[sg(H), sg(XLEV, H), sg(H), sg(XLEV - 1, H), sg(H), sg(H), sg(H), sg(H), sg(H),
                        sh(H), sh(H), sh(H),
                        sg(6, HH), sg(HH), sg(HH), sg(HH), sg(HH), sg(HH),
                        sg(3, HH), sg(3, HH), sg(HH), sg(HH), sg(3, HH), sg(HH),
                        tv(9), tv(8), tv(8), tv(8), tv(8), tv(XLEV), tv(), tv(), tv(), tv(), tv(), tv(), sg(),
                        dma((24,)), dma((HH,)), dma((HH,)), dma((6, HH)), dma((5, HH)), dma((HH,)),
                        dma((HH,)), dma((HH,)), dma((3, HH)), dma((3, HH)), dma((HH,)), dma((HH,))]
                       + [dma((8,))] * 8,
        compiler_params=pltpu.CompilerParams(collective_id=0, has_side_effects=True,
                                             vmem_limit_bytes=62 * 1024 * 1024),
        name="fused",
    )(q, k, v, g, gain, decay)


def per_device(queries, keys_in, value_input, level_gain, decay_log, out_grad):
    return tuple(fused(queries, keys_in, value_input, out_grad, level_gain, decay_log))


def solution(mesh):
    tokens = P(("seq", "ctx"), None)
    gains = P(None, None, ("seq", "ctx"))
    decays = P(None, ("seq", "ctx"))
    return jax.shard_map(
        per_device,
        mesh=mesh,
        in_specs=(tokens, tokens, tokens, gains, decays, tokens),
        out_specs=(tokens, tokens, tokens, tokens, gains, decays),
        check_vma=False,
    )
```

time: 120 us -> 99 us (0.82)
  Pallas kernels: 117 us -> 91.3 us
  local copies, waits for them, and re-layouts: 1.3 us -> 6.69 us
    pallas_call x4 -> x1, Pallas kernels: 117 us -> 91.3 us  [fused(): pl.pallas_call(fused_kernel, in_specs=[vm] * 6, out_specs=[vm] * 6, out_s...]
    unnamed x1 -> x16, local copies, waits for them, and re-layouts: 1.3 us -> 6.69 us
where the time goes in v4:
time: 99 us; the launch traced here: 98.7 us
  Pallas kernels  91.3 us (92%)
  local copies, waits for them, and re-layouts  6.69 us (7%)
    pallas_call x1, Pallas kernels, fused(): pl.pallas_call(fused_kernel, in_specs=[vm] * 6, out_specs=[vm] * 6, out_s...  91.3 us
    unnamed x16, local copies, waits for them, and re-layouts  6.69 us

profile of v4, /device:TPU:1, one launch (start us, length us, event | category | flops | bytes accessed | tf_op | source)
XLA Modules:
  0.0 98.7 jit_solution(12271357421045808928)
XLA Ops:
  0.6 91.3 %fused.1 = (bf16[128,2048]{1,0:T(8,128)(2,1)}, bf16[128,2048]{1,0:T(8,128)(2,1)}, bf16[128,2048]{1,0:T(8,128)(2,1)}, bf16[128,2048]{1,0:T(8,128)(2,1)}, f32[14,16,128]{2,1,0:T(8,128)}, /*index=5*/f32[16,128]{1,0:T(8,128)}) custom-call(bf16[128,2048]{1,0:T(8,128)(2,1)} %q_ref.1, bf16[128,2048]{1,0:T(8,128)(2,1)} %k_ref.1, bf16[128,2048]{1,0:T(8,128)(2,1)} %v_ref.1, ...), custom_call_target="tpu_custom_call" | custom-call | tf_op jit(solution)/shard_map/fused/pallas_call | solution.py:668
  92.0 0.0 copy-start.2
  92.0 1.9 %copy.18 = bf16[128,2048]{1,0:T(8,128)(2,1)} copy(bf16[128,2048]{1,0:T(8,128)(2,1)} %get-tuple-element.12) | data formatting | bytes 1048576
  93.9 0.0 copy-done.2
  93.9 0.0 copy-start.1
  93.9 0.8 copy.19
  94.7 0.4 copy-done.1
  95.2 0.0 copy-start
  95.2 0.8 copy.20
  96.0 0.4 copy-done
  96.4 0.0 copy-start.3
  96.4 0.8 copy.21
  97.2 0.2 copy-done.3
  97.4 0.0 copy-start.4
  97.4 0.6 copy.22
  98.0 0.0 copy-done.4
  98.1 0.6 copy.23
Async XLA Ops:
  92.0 2.0 %copy-start.2 = (bf16[128,2048]{1,0:T(8,128)(2,1)S(1)}, bf16[128,2048]{1,0:T(8,128)(2,1)}, u32[]{:S(2)}) copy-start(bf16[128,2048]{1,0:T(8,128)(2,1)} %get-tuple-element.13) | copy-start | bytes 1572868
  93.9 1.2 %copy-start.1 = (bf16[128,2048]{1,0:T(8,128)(2,1)S(1)}, bf16[128,2048]{1,0:T(8,128)(2,1)}, u32[]{:S(2)}) copy-start(bf16[128,2048]{1,0:T(8,128)(2,1)} %get-tuple-element.14) | copy-start | bytes 1572868
  95.2 1.2 %copy-start = (bf16[128,2048]{1,0:T(8,128)(2,1)S(1)}, bf16[128,2048]{1,0:T(8,128)(2,1)}, u32[]{:S(2)}) copy-start(bf16[128,2048]{1,0:T(8,128)(2,1)} %get-tuple-element.15) | copy-start | bytes 1572868
  96.4 1.0 %copy-start.3 = (f32[14,16,128]{2,1,0:T(8,128)S(1)}, f32[14,16,128]{2,1,0:T(8,128)}, u32[]{:S(2)}) copy-start(f32[14,16,128]{2,1,0:T(8,128)} %get-tuple-element.16) | copy-start | bytes 344068
  97.4 0.7 copy-start.4

commit v5 on v4

--- a/solution.py
+++ b/solution.py
@@ -63,13 +63,14 @@
     return acc
 
 
-def fused_kernel(q_ref, k_ref, v_ref, g_ref, gain_ref, decay_ref,
+def fused_kernel(q_in, k_in, v_in, g_in, gain_in, decay_in,
                  o_ref, dq_ref, dk_ref, dv_ref, dgain_ref, ddecay_ref,
                  st, g_st, b0, bk, ds, oacc, dqacc, dkacc, dvacc, qt_sc, kt_sc, gt_sc,
                  rg, cbuf, mbuf, rbuf, pbuf, qbuf, ebuf, fbuf, abuf, bbuf, ybuf, xbuf,
-                 tt, rowt, zt, rowf, zf, off, rsum, own, run_sc, row_sc, flux, zflux_sum, col_sc,
+                 tt, rowt, zt, rowf, off, rsum, own, run_sc, row_sc, flux, flow_sc, col_sc,
                  ssem, rx1, rx1b, rx2, rx4, rx5, ry1, ry2, rz, re, ra, rb,
-                 trs, trr, tzs, tzr, frs, frr, fzs, fzr):
+                 trs, trr, tzs, tzr, frs, frr,
+                 q_ref, k_ref, v_ref, g_ref, gain_ref, decay_ref, insem):
     seq = lax.axis_index("seq")
     c, b, y, z = coords()
     r = lax.rem(c, 8)
@@ -84,19 +85,52 @@
     yhi = y >= 2
     zb = [lax.rem(z, 2) == 1, lax.rem(z // 2, 2) == 1, z >= 4]
     row_peer = [z * 8 + lax.rem(r + i, 8) for i in range(8)]
-    z_peer = [lax.rem(z + i, 8) * 8 + r for i in range(8)]
     row_from = [lax.rem(r - i + 8, 8) for i in range(8)]
-    z_from = [lax.rem(z - i + 8, 8) for i in range(8)]
-
+
+    loads = [pltpu.make_async_copy(src, dst, insem.at[i]) for i, (src, dst) in enumerate((
+        (decay_in, decay_ref), (k_in, k_ref), (v_in, v_ref), (q_in, q_ref), (g_in, g_ref), (gain_in, gain_ref)))]
+    for load in loads:
+        load.start()
     barrier = pltpu.get_barrier_semaphore()
     for i in range(1, 8):
         pl.semaphore_signal(barrier, inc=1, device_id=(seq, row_peer[i]), device_id_type=MESH)
-        pl.semaphore_signal(barrier, inc=1, device_id=(seq, z_peer[i]), device_id_type=MESH)
+
+    @pl.when(z < 7)
+    def _():
+        pl.semaphore_signal(barrier, inc=1, device_id=(seq, up), device_id_type=MESH)
+
+    @pl.when(z > 0)
+    def _():
+        pl.semaphore_signal(barrier, inc=1, device_id=(seq, dn), device_id_type=MESH)
+
+    loads[0].wait()
     run, tot = running_sums(decay_ref[...])
     run_sc[...] = run
     own[...] = tot
     dgain_ref[...] = jnp.zeros((LVL_IN + XLEV, H, N), F32)
-    pl.semaphore_wait(barrier, 14)
+    col_sc[...] = jnp.zeros((N, N), F32)
+    flow_sc[...] = jnp.zeros((H, N), F32)
+
+    def cols(h):
+        return pl.ds(pl.multiple_of(h * N, N), N)
+
+    def row(ref, h):
+        return ref[pl.ds(h, 1), :]
+
+    def make_state(h):
+        kt = jnp.transpose(k_ref[:, cols(h)].astype(F32))
+        kt_sc[h] = kt.astype(BF16)
+        v = v_ref[:, cols(h)]
+        st[h] = mm(wide(kt * jnp.exp(row(own, h) - row(run_sc, h))), jnp.concatenate([v, v], axis=0))
+
+    def states_first(h, carry):
+        make_state(theirs + h)
+        return carry
+
+    loads[1].wait()
+    loads[2].wait()
+    lax.fori_loop(0, HH, states_first, 0)
+    pl.semaphore_wait(barrier, 7 + jnp.minimum(z, 1) + jnp.minimum(7 - z, 1))
 
     def copy(src, dst, send, recv, who):
         return pltpu.make_async_remote_copy(src_ref=src, dst_ref=dst, send_sem=send, recv_sem=recv,
@@ -136,16 +170,13 @@
         return copy(bbuf.at[h], ybuf.at[1, h], ssem.at[23], rb.at[h], yn)
 
     def rtot(i):
-        return copy(own, rowt.at[i], trs.at[i], trr.at[i], row_peer[i])
-
-    def ztot(i):
-        return copy(rsum, zt.at[i], tzs.at[i], tzr.at[i], z_peer[i])
+        return copy(own, rowt.at[i], trs.at[i], trr.at[i], z * 8 + lax.rem(r + i, 8))
+
+    def ztot():
+        return copy(rsum, zt, tzs.at[0], tzr.at[0], up)
 
     def rflux(i):
         return copy(flux, rowf.at[i], frs.at[i], frr.at[i], row_peer[i])
-
-    def zflux(i):
-        return copy(zflux_sum, zf.at[i], fzs.at[i], fzr.at[i], z_peer[i])
 
     setbits = [None, yodd, yhi, zb[0], zb[1], zb[2]]
 
@@ -155,20 +186,11 @@
             return carry
         lax.fori_loop(0, HH, body, 0)
 
-    for i in range(1, 8):
+    rtot(jnp.where(b == 0, 1, 7)).start()
+    each(lambda h: x1(h).start())
+    rtot(jnp.where(b == 0, 7, 1)).start()
+    for i in range(2, 7):
         rtot(i).start()
-
-    def cols(h):
-        return pl.ds(pl.multiple_of(h * N, N), N)
-
-    def row(ref, h):
-        return ref[pl.ds(h, 1), :]
-
-    def make_state(h):
-        kt = jnp.transpose(k_ref[:, cols(h)].astype(F32))
-        kt_sc[h] = kt.astype(BF16)
-        v = v_ref[:, cols(h)]
-        st[h] = mm(wide(kt * jnp.exp(row(own, h) - row(run_sc, h))), jnp.concatenate([v, v], axis=0))
 
     def make_turned(h):
         qt_sc[h] = flip(q_ref[:, cols(h)])
@@ -179,10 +201,6 @@
         scale = gain_ref[LVL_IN + j, pl.ds(h, 1), :] * jnp.exp(row(run_sc, h))
         g_st[j, h] = mm(wide(qt_sc[h].astype(F32) * scale), jnp.concatenate([g, g], axis=0))
 
-    def state_theirs(h):
-        make_state(theirs + h)
-        x1(h).start()
-
     def state_mine(h):
         make_state(mine + h)
 
@@ -190,7 +208,6 @@
         def _():
             x1b(h).start()
 
-    each(state_theirs)
     each(state_mine)
 
     @pl.when(z == 7)
@@ -199,37 +216,50 @@
             ebuf[2, h] = jnp.zeros((N, N), F32)
         each(zero)
 
-    for i in range(1, 8):
-        rtot(i).wait_recv()
-    parts = [own[...]] + [rowt[i] for i in range(1, 8)]
-    rows = pick(parts, lambda i: row_from[i] >= 0)
-    rsum[...] = rows
-    for i in range(1, 8):
-        ztot(i).start()
-    core0 = pick(parts, lambda i: row_from[i] == 2 * y)
-    core1 = pick(parts, lambda i: row_from[i] == 2 * y + 1)
-    tt[0] = core0
-    tt[1] = core1
-    tt[2] = pick(parts, lambda i: row_from[i] // 2 == 2 * (y // 2) + 1)
-    tt[3] = pick(parts, lambda i: row_from[i] >= 4)
-    tt[4] = rows
-    tt[5] = pick(parts, lambda i: row_from[i] < 2 * y)
-    tt[6] = pick(parts, lambda i: jnp.logical_and(row_from[i] >= 4, row_from[i] < 2 * y))
-    tt[7] = jnp.zeros((H, N), F32)
-    off[0] = jnp.zeros((H, N), F32)
-    off[1] = jnp.where(b == 1, core0, 0.0)
-    off[2] = pick(parts, lambda i: jnp.logical_and(row_from[i] >= 4 * (y // 2), row_from[i] < r))         if False else jnp.where(b == 1, core0, 0.0) + pick(
-            parts, lambda i: jnp.logical_and(row_from[i] // 2 == y - 1, yodd))
-    off3 = pick(parts, lambda i: row_from[i] < r)
-    off[3] = off3
+    pair_slot = jnp.where(b == 0, 7, 1)
+    rtot(pair_slot).wait_recv()
+    tt[0] = jnp.where(b == 0, own[...], rowt[pair_slot])
+    tt[1] = jnp.where(b == 0, rowt[pair_slot], own[...])
+
+    def row_tables():
+        rtot(8 - pair_slot).wait_recv()
+        for i in range(2, 7):
+            rtot(i).wait_recv()
+        parts = [own[...]] + [rowt[i] for i in range(1, 8)]
+        rows = pick(parts, lambda i: row_from[i] >= 0)
+        rsum[1] = rows
+        tt[2] = pick(parts, lambda i: row_from[i] // 2 == 2 * (y // 2) + 1)
+        tt[3] = pick(parts, lambda i: row_from[i] >= 4)
+        tt[4] = rows
+        tt[5] = pick(parts, lambda i: row_from[i] < 2 * y)
+        tt[6] = pick(parts, lambda i: jnp.logical_and(row_from[i] >= 4, row_from[i] < 2 * y))
+        tt[7] = jnp.zeros((H, N), F32)
+        off[0] = jnp.zeros((H, N), F32)
+        off[1] = jnp.where(b == 1, tt[0], 0.0)
+        off[2] = pick(parts, lambda i: jnp.logical_and(row_from[i] >= 4 * (y // 2), row_from[i] < r))
+        off[3] = pick(parts, lambda i: row_from[i] < r)
+
+    zq = lax.rem(z, 4)
 
     def z_tables():
-        for i in range(1, 8):
-            ztot(i).wait_recv()
-        zp = [tt[4]] + [zt[i] for i in range(1, 8)]
-        tt[8] = pick(zp, lambda i: jnp.logical_and(z_from[i] >= z - 1, z_from[i] <= z))
-        off[4] = off[3] + pick(zp, lambda i: jnp.logical_and(z_from[i] >= 2 * (z // 2), z_from[i] < z))
-        off[5] = off[3] + pick(zp, lambda i: jnp.logical_and(z_from[i] >= 4 * (z // 4), z_from[i] < z))
+        @pl.when(zq == 0)
+        def _():
+            zt[...] = jnp.zeros((2, H, N), F32)
+
+        @pl.when(zq > 0)
+        def _():
+            ztot().wait_recv()
+
+        below, last = zt[0], zt[1]
+        tt[8] = tt[4] + last
+        tt[9] = tt[4] + below
+        off[4] = off[3] + jnp.where(zb[0], last, 0.0)
+        off[5] = off[3] + below
+        rsum[0] = tt[4] + below
+
+        @pl.when(zq < 3)
+        def _():
+            ztot().start()
 
     def tb(k, h):
         return tt[k, pl.ds(mine + h, 1), :]
@@ -460,6 +490,26 @@
         t_i = lax.broadcasted_iota(jnp.int32, (N, N), 1)
         col_sc[...] = jnp.where(t_i == h, jnp.sum(v.astype(F32) * dv, axis=1, keepdims=True), col_sc[...])
 
+    def flow(h):
+        acc = main_state(h) * ebuf[d_slot, h]
+        flow_sc[pl.ds(mine + h, 1), :] = jnp.sum(acc, axis=0, keepdims=True)
+
+        def more(j, k):
+            term = jnp.sum(bk[j, mine + h] * ebuf[j - 2, h], axis=0, keepdims=True)
+            flow_sc[pl.ds(mine + h, 1), :] = flow_sc[pl.ds(mine + h, 1), :] + jnp.exp(tb(k, h)) * term
+
+        @pl.when(jnp.logical_and(zb[1], jnp.logical_not(zb[0])))
+        def _():
+            more(3, 4)
+
+        @pl.when(jnp.logical_and(z > 3, z < 7))
+        def _():
+            more(4, 9)
+
+    def main_state(h):
+        upper = jnp.where(z == 3, qbuf[h], pbuf[h])
+        return jnp.where(zb[0], upper, rbuf[h])
+
     def tail_own(h):
         tail_terms(mine + h)
 
@@ -523,8 +573,10 @@
         grads_early(i)
         return carry
 
-    col_sc[...] = jnp.zeros((N, N), F32)
     each(f1)
+    row_tables()
+    for load in loads[3:]:
+        load.wait()
     lax.fori_loop(0, H, early, 0)
 
     @pl.when(z == 7)
@@ -546,7 +598,7 @@
             def _():
                 fn(h)
 
-        @pl.when(t == 5)
+        @pl.when(t == 2 * zq + 1)
         def _():
             z_tables()
 
@@ -564,6 +616,7 @@
         stage(grads_late, 0, count=H)
         stage(d_ready, B0 + d_lag, in_cond[0])
         stage(a_send, B0 + d_lag)
+        stage(flow, B0 + d_lag + 1)
         stage(ya, B0 + d_lag + hop(1))
         stage(yb, B0 + d_lag + hop(2))
         stage(tail_own, B0 + d_lag + hop(2) + 1)
@@ -588,35 +641,26 @@
     da = row_sc[...] - jnp.transpose(col_sc[...])[0:H, :]
     s_i = lax.broadcasted_iota(jnp.int32, (N, N), 0)
     t_i = lax.broadcasted_iota(jnp.int32, (N, N), 1)
-    flux[...] = lax.dot_general(da, jnp.ones((N, N), F32), NN, precision=lax.Precision.HIGHEST,
-                                preferred_element_type=F32)
+    ones = jnp.ones((N, N), F32)
+
+    def dot01(a, m):
+        return lax.dot_general(a, m, NN, precision=lax.Precision.HIGHEST, preferred_element_type=F32)
+
+    flux[0] = dot01(da, ones)
+    flux[1] = dot01(flow_sc[...], ones)
     for i in range(1, 8):
         rflux(i).start()
 
-    def put_out(h):
+    def put(h, carry):
         o_ref[:, cols(h)] = oacc[h].astype(BF16)
         dq_ref[:, cols(h)] = jnp.transpose(dqacc[h]).astype(BF16)
-
-    def put(h, carry):
-        put_out(h)
         return carry
 
-    lax.fori_loop(0, HH, put, 0)
-    total = flux[...]
-    after = lax.dot_general(da, (s_i >= t_i).astype(F32), NN, precision=lax.Precision.HIGHEST,
-                            preferred_element_type=F32)
+    lax.fori_loop(0, H, put, 0)
+    after = dot01(da, (s_i >= t_i).astype(F32)) + flux[1]
     for i in range(1, 8):
         rflux(i).wait_recv()
-        val = rowf[i]
-        total = total + val
-        after = after + jnp.where(row_from[i] > r, val, 0.0)
-    zflux_sum[...] = total
-    for i in range(1, 8):
-        zflux(i).start()
-    lax.fori_loop(HH, H, put, 0)
-    for i in range(1, 8):
-        zflux(i).wait_recv()
-        after = after + jnp.where(z_from[i] > z, zf[i], 0.0)
+        after = after + rowf[i, 1] + jnp.where(row_from[i] > r, rowf[i, 0], 0.0)
     ddecay_ref[...] = after
 
     def all_of(src, dst, send, recv):
@@ -653,9 +697,11 @@
         pl.when(zb[j])(esent)
     for i in range(1, 8):
         rtot(i).wait_send()
-        ztot(i).wait_send()
         rflux(i).wait_send()
-        zflux(i).wait_send()
+
+    @pl.when(zq < 3)
+    def _():
+        ztot().wait_send()
 
 
 def fused(q, k, v, g, gain, decay):
@@ -667,7 +713,7 @@
     wide_out = jax.ShapeDtypeStruct((N, H * N), BF16)
     return pl.pallas_call(
         fused_kernel,
-        in_specs=[vm] * 6,
+        in_specs=[pl.BlockSpec(memory_space=pltpu.MemorySpace.HBM)] * 6,
         out_specs=[vm] * 6,
         out_shape=[wide_out, wide_out, wide_out, wide_out,
                    jax.ShapeDtypeStruct((LVL_IN + XLEV, H, N), F32),
@@ -676,18 +722,40 @@
                         sh(H), sh(H), sh(H),
                         sg(6, HH), sg(HH), sg(HH), sg(HH), sg(HH), sg(HH),
                         sg(3, HH), sg(3, HH), sg(HH), sg(HH), sg(3, HH), sg(HH),
-                        tv(9), tv(8), tv(8), tv(8), tv(8), tv(XLEV), tv(), tv(), tv(), tv(), tv(), tv(), sg(),
+                        tv(10), tv(8), tv(2), tv(8, 2), tv(XLEV), tv(2), tv(), tv(), tv(), tv(2), tv(), sg(),
                         dma((24,)), dma((HH,)), dma((HH,)), dma((6, HH)), dma((5, HH)), dma((HH,)),
                         dma((HH,)), dma((HH,)), dma((3, HH)), dma((3, HH)), dma((HH,)), dma((HH,))]
-                       + [dma((8,))] * 8,
+                       + [dma((8,))] * 6
+                       + [pltpu.VMEM((N, H * N), BF16)] * 4
+                       + [tv(LVL_IN + XLEV), tv(), dma((6,))],
         compiler_params=pltpu.CompilerParams(collective_id=0, has_side_effects=True,
-                                             vmem_limit_bytes=62 * 1024 * 1024),
+                                             vmem_limit_bytes=44 * 1024 * 1024),
         name="fused",
     )(q, k, v, g, gain, decay)
 
 
+def finish_kernel(*refs):
+    ins, outs, sem = refs[:6], refs[6:12], refs[12]
+    for i in range(6):
+        pltpu.make_async_copy(ins[i], outs[i], sem.at[i]).start()
+    for i in range(6):
+        pltpu.make_async_copy(ins[i], outs[i], sem.at[i]).wait()
+
+
+def finish(*arrays):
+    return pl.pallas_call(
+        finish_kernel,
+        in_specs=[pl.BlockSpec(memory_space=pltpu.VMEM)] * 6,
+        out_specs=[pl.BlockSpec(memory_space=pl.ANY)] * 6,
+        out_shape=[jax.ShapeDtypeStruct(a.shape, a.dtype) for a in arrays],
+        scratch_shapes=[pltpu.SemaphoreType.DMA((6,))],
+        compiler_params=pltpu.CompilerParams(vmem_limit_bytes=8 * 1024 * 1024),
+        name="finish",
+    )(*arrays)
+
+
 def per_device(queries, keys_in, value_input, level_gain, decay_log, out_grad):
-    return tuple(fused(queries, keys_in, value_input, out_grad, level_gain, decay_log))
+    return tuple(finish(*fused(queries, keys_in, value_input, out_grad, level_gain, decay_log)))
 
 
 def solution(mesh):

time: 99 us -> 89.8 us (0.907)
  Pallas kernels: 91.3 us -> 83.1 us
    pallas_call x1 -> x2, Pallas kernels: 91.3 us -> 83.1 us  [the longest x1 81.7 us: fused(): pl.pallas_call(fused_kernel, in_specs=[pl.BlockSpec(memory_space=pltpu.Me...]
    unnamed x16 -> x12, local copies, waits for them, and re-layouts: 6.69 us -> 5.75 us
where the time goes in v5:
time: 89.8 us; the launch traced here: 89.5 us
  Pallas kernels  83.1 us (93%)
  local copies, waits for them, and re-layouts  5.75 us (6%)
    pallas_call x1, Pallas kernels, fused(): pl.pallas_call(fused_kernel, in_specs=[pl.BlockSpec(memory_space=pltpu.Me...  81.7 us
    unnamed x12, local copies, waits for them, and re-layouts  5.75 us

profile of v5, /device:TPU:1, one launch (start us, length us, event | category | flops | bytes accessed | tf_op | source)
XLA Modules:
  0.0 89.5 jit_solution(481901512812359151)
XLA Ops:
  0.6 0.0 copy-start
  0.6 1.0 %copy-done = bf16[128,2048]{1,0:T(8,128)(2,1)S(1)} copy-done((bf16[128,2048]{1,0:T(8,128)(2,1)S(1)}, bf16[128,2048]{1,0:T(8,128)(2,1)}, u32[]{:S(2)}) %copy-start) | copy-done | bytes 524312
  1.7 0.0 copy-start.1
  1.7 1.0 %copy-done.1 = bf16[128,2048]{1,0:T(8,128)(2,1)S(1)} copy-done((bf16[128,2048]{1,0:T(8,128)(2,1)S(1)}, bf16[128,2048]{1,0:T(8,128)(2,1)}, u32[]{:S(2)}) %copy-start.1) | copy-done | bytes 524312
  2.7 0.0 copy-start.2
  2.7 1.0 %copy-done.2 = bf16[128,2048]{1,0:T(8,128)(2,1)S(1)} copy-done((bf16[128,2048]{1,0:T(8,128)(2,1)S(1)}, bf16[128,2048]{1,0:T(8,128)(2,1)}, u32[]{:S(2)}) %copy-start.2) | copy-done | bytes 524312
  3.8 0.0 copy-start.3
  3.8 1.0 %copy-done.3 = bf16[128,2048]{1,0:T(8,128)(2,1)S(1)} copy-done((bf16[128,2048]{1,0:T(8,128)(2,1)S(1)}, bf16[128,2048]{1,0:T(8,128)(2,1)}, u32[]{:S(2)}) %copy-start.3) | copy-done | bytes 524312
  4.8 0.0 copy-start.4
  4.8 0.9 %copy-done.4 = f32[14,16,128]{2,1,0:T(8,128)S(1)} copy-done((f32[14,16,128]{2,1,0:T(8,128)S(1)}, f32[14,16,128]{2,1,0:T(8,128)}, u32[]{:S(2)}) %copy-start.4) | copy-done | bytes 114712
  5.7 0.0 copy-start.5
  5.7 0.7 copy-done.5
  6.4 81.7 %fused.1 = (bf16[128,2048]{1,0:T(8,128)(2,1)S(1)}, bf16[128,2048]{1,0:T(8,128)(2,1)S(1)}, bf16[128,2048]{1,0:T(8,128)(2,1)S(1)}, bf16[128,2048]{1,0:T(8,128)(2,1...) custom-call(bf16[128,2048]{1,0:T(8,128)(2,1)S(1)} %copy-done, bf16[128,2048]{1,0:T(8,128)(2,1)S(1)} %copy-done.1, ...), custom_call_target="tpu_custom_call" | custom-call | tf_op jit(solution)/shard_map/fused/pallas_call | solution.py:714
  88.1 1.4 %finish.1 = (bf16[128,2048]{1,0:T(8,128)(2,1)}, bf16[128,2048]{1,0:T(8,128)(2,1)}, bf16[128,2048]{1,0:T(8,128)(2,1)}, bf16[128,2048]{1,0:T(8,128)(2,1)}, f32[14,16,128]{2,1,0:T(8,128)}, /*index=5*/f32[16,128]{1,0:T(8,128)}) custom-call(bf16[128,2048]{1,0:T(8,128)(2,1)S(1)} %get-tuple-element.12.refs_0_, bf16[128,2048]{1,0:T(8,128)(2,1)S(1)} %get-tuple-element.13.refs_1_, ...), custom_call_target="tpu_custom_call" | custom-call | tf_op jit(solution)/shard_map/finish/pallas_call | solution.py:746
Async XLA Ops:
  0.6 1.0 %copy-start = (bf16[128,2048]{1,0:T(8,128)(2,1)S(1)}, bf16[128,2048]{1,0:T(8,128)(2,1)}, u32[]{:S(2)}) copy-start(bf16[128,2048]{1,0:T(8,128)(2,1)} %q_in.1) | copy-start | bytes 1572868
  1.7 1.0 %copy-start.1 = (bf16[128,2048]{1,0:T(8,128)(2,1)S(1)}, bf16[128,2048]{1,0:T(8,128)(2,1)}, u32[]{:S(2)}) copy-start(bf16[128,2048]{1,0:T(8,128)(2,1)} %k_in.1) | copy-start | bytes 1572868
  2.7 1.0 %copy-start.2 = (bf16[128,2048]{1,0:T(8,128)(2,1)S(1)}, bf16[128,2048]{1,0:T(8,128)(2,1)}, u32[]{:S(2)}) copy-start(bf16[128,2048]{1,0:T(8,128)(2,1)} %v_in.1) | copy-start | bytes 1572868
  3.8 1.0 %copy-start.3 = (bf16[128,2048]{1,0:T(8,128)(2,1)S(1)}, bf16[128,2048]{1,0:T(8,128)(2,1)}, u32[]{:S(2)}) copy-start(bf16[128,2048]{1,0:T(8,128)(2,1)} %g_in.1) | copy-start | bytes 1572868
  4.8 0.9 %copy-start.4 = (f32[14,16,128]{2,1,0:T(8,128)S(1)}, f32[14,16,128]{2,1,0:T(8,128)}, u32[]{:S(2)}) copy-start(f32[14,16,128]{2,1,0:T(8,128)} %gain_in.1) | copy-start | bytes 344068
  5.7 0.7 copy-start.5

commit v6 on v5

--- a/solution.py
+++ b/solution.py
@@ -129,7 +129,12 @@
 
     loads[1].wait()
     loads[2].wait()
-    lax.fori_loop(0, HH, states_first, 0)
+    last_row = z == 7
+
+    @pl.when(jnp.logical_not(last_row))
+    def _():
+        lax.fori_loop(0, HH, states_first, 0)
+
     pl.semaphore_wait(barrier, 7 + jnp.minimum(z, 1) + jnp.minimum(7 - z, 1))
 
     def copy(src, dst, send, recv, who):
@@ -187,7 +192,11 @@
         lax.fori_loop(0, HH, body, 0)
 
     rtot(jnp.where(b == 0, 1, 7)).start()
-    each(lambda h: x1(h).start())
+
+    @pl.when(jnp.logical_not(last_row))
+    def _():
+        each(lambda h: x1(h).start())
+
     rtot(jnp.where(b == 0, 7, 1)).start()
     for i in range(2, 7):
         rtot(i).start()
@@ -208,7 +217,43 @@
         def _():
             x1b(h).start()
 
-    each(state_mine)
+    @pl.when(jnp.logical_not(last_row))
+    def _():
+        each(state_mine)
+
+    for load in loads[3:]:
+        load.wait()
+
+    def all_heads(fn):
+        def body(i, carry):
+            fn(i)
+            return carry
+        lax.fori_loop(0, H, body, 0)
+
+    def grad_and_send(j):
+        def go(i):
+            h = lax.rem(theirs + i, H)
+            make_grad(j, h)
+
+            @pl.when(i < HH)
+            def _():
+                x2(j, i).start()
+        return go
+
+    def turned_and_top():
+        all_heads(make_turned)
+
+        @pl.when(setbits[5])
+        def _():
+            all_heads(grad_and_send(5))
+
+    @pl.when(last_row)
+    def _():
+        def partner_head(h):
+            make_turned(theirs + h)
+            grad_and_send(5)(h)
+        each(partner_head)
+
 
     @pl.when(z == 7)
     def _():
@@ -517,19 +562,6 @@
         copy(ds.at[theirs + h], ds.at[theirs + h], ssem.at[13], rx5.at[h], part).wait_recv()
         tail_terms(theirs + h)
 
-    def grads_early(i):
-        h = lax.rem(theirs + i, H)
-        make_turned(h)
-
-        for j in (5, 4, 3):
-            @pl.when(setbits[j])
-            def _(j=j):
-                make_grad(j, h)
-
-                @pl.when(i < HH)
-                def _():
-                    x2(j, i).start()
-
     def grads_late(i):
         h = lax.rem(theirs + i, H)
         for j in (2, 1, 0):
@@ -569,23 +601,39 @@
         fbuf[0, h] = chip_grad(3, h, 5) - chip_grad(4, h, 5)
         emsg(0, h).start()
 
-    def early(i, carry):
-        grads_early(i)
-        return carry
-
-    each(f1)
+    @pl.when(jnp.logical_not(last_row))
+    def _():
+        each(f1)
+
     row_tables()
-    for load in loads[3:]:
-        load.wait()
-    lax.fori_loop(0, H, early, 0)
-
-    @pl.when(z == 7)
-    def _():
-        each(e_send(2))
-        each(e_send(1))
-        each(e_send(0))
-
-    B0 = 2
+
+    @pl.when(last_row)
+    def _():
+        def own_head(h):
+            make_turned(mine + h)
+            make_grad(5, mine + h)
+            e_send(2)(h)
+        each(own_head)
+        lax.fori_loop(0, HH, states_first, 0)
+        each(lambda h: x1(h).start())
+        each(state_mine)
+        each(f1)
+
+    @pl.when(jnp.logical_not(last_row))
+    def _():
+        turned_and_top()
+
+    for j in (4, 3):
+        @pl.when(setbits[j])
+        def _(j=j):
+            all_heads(grad_and_send(j))
+
+        @pl.when(last_row)
+        def _(j=j):
+            each(e_send(j - 3))
+
+    B0 = 0
+    F0 = 0
 
     def tick(t, carry):
         def stage(fn, lag, cond=None, count=HH):
@@ -606,17 +654,17 @@
         stage(e_send(2), B0 + e5_lag, z > 3)
         stage(e_wait(1), B0 + e4_in)
         stage(e_send(1), B0 + e4_out)
-        stage(f2, 0)
-        stage(f3, hop(2) - hop(1))
-        stage(f4, hop(3) - hop(1), zb[0])
-        stage(f5, hop(4) - hop(1) + jnp.where(zb[0], hop(5) - hop(4), 0), zb[1])
+        stage(f2, F0)
+        stage(f3, F0 + hop(2) - hop(1))
+        stage(f4, F0 + hop(3) - hop(1), zb[0])
+        stage(f5, F0 + hop(4) - hop(1) + jnp.where(zb[0], hop(5) - hop(4), 0), zb[1])
         stage(f7, f7_lag - hop(1))
         stage(delta_send, B0 + e3_out, z == 3)
         stage(e_send(0), B0 + e3_out, z != 3)
         stage(grads_late, 0, count=H)
         stage(d_ready, B0 + d_lag, in_cond[0])
         stage(a_send, B0 + d_lag)
-        stage(flow, B0 + d_lag + 1)
+        stage(flow, B0 + d_lag + 4)
         stage(ya, B0 + d_lag + hop(1))
         stage(yb, B0 + d_lag + hop(2))
         stage(tail_own, B0 + d_lag + hop(2) + 1)
@@ -731,7 +779,7 @@
         compiler_params=pltpu.CompilerParams(collective_id=0, has_side_effects=True,
                                              vmem_limit_bytes=44 * 1024 * 1024),
         name="fused",
-    )(q, k, v, g, gain, decay)
+    )(*(pltpu.with_memory_space_constraint(a, pltpu.MemorySpace.HBM) for a in (q, k, v, g, gain, decay)))
 
 
 def finish_kernel(*refs):

time: 89.8 us -> 80 us (0.89)
  local copies, waits for them, and re-layouts: 5.75 us -> 0 us
  Pallas kernels: 83.1 us -> 79.2 us
    unnamed x12 -> x0, local copies, waits for them, and re-layouts: 5.75 us -> none
    pallas_call x1, Pallas kernels: 81.7 us -> 77.8 us  [fused(): pl.pallas_call(fused_kernel, in_specs=[pl.BlockSpec(memory_space=pltpu.Me...]
where the time goes in v6:
time: 80 us; the launch traced here: 79.9 us
  Pallas kernels  79.2 us (99%)
    pallas_call x1, Pallas kernels, fused(): pl.pallas_call(fused_kernel, in_specs=[pl.BlockSpec(memory_space=pltpu.Me...  77.8 us

profile of v6, /device:TPU:1, one launch (start us, length us, event | category | flops | bytes accessed | tf_op | source)
XLA Modules:
  0.0 79.9 jit_solution(12485342525571371482)
XLA Ops:
  0.6 77.8 %fused.1 = (bf16[128,2048]{1,0:T(8,128)(2,1)S(1)}, bf16[128,2048]{1,0:T(8,128)(2,1)S(1)}, bf16[128,2048]{1,0:T(8,128)(2,1)S(1)}, bf16[128,2048]{1,0:T(8,128)(2,1...) custom-call(bf16[128,2048]{1,0:T(8,128)(2,1)} %q_in.1, bf16[128,2048]{1,0:T(8,128)(2,1)} %k_in.1, ...), custom_call_target="tpu_custom_call" | custom-call | tf_op jit(solution)/shard_map/fused/pallas_call | solution.py:762
  78.5 1.4 %finish.1 = (bf16[128,2048]{1,0:T(8,128)(2,1)}, bf16[128,2048]{1,0:T(8,128)(2,1)}, bf16[128,2048]{1,0:T(8,128)(2,1)}, bf16[128,2048]{1,0:T(8,128)(2,1)}, f32[14,16,128]{2,1,0:T(8,128)}, /*index=5*/f32[16,128]{1,0:T(8,128)}) custom-call(bf16[128,2048]{1,0:T(8,128)(2,1)S(1)} %get-tuple-element.12.refs_0_, bf16[128,2048]{1,0:T(8,128)(2,1)S(1)} %get-tuple-element.13.refs_1_, ...), custom_call_target="tpu_custom_call" | custom-call | tf_op jit(solution)/shard_map/finish/pallas_call | solution.py:794

commit v7 on v6

--- a/solution.py
+++ b/solution.py
@@ -677,10 +677,10 @@
         stage(level_own(4), 12, setbits[4])
         stage(level_own(5), f7_lag - hop(1) + 1, setbits[5])
         stage(level_other(0), 20, b == 1)
-        stage(level_other(1), 15, setbits[1])
-        stage(level_other(2), 17, setbits[2])
-        stage(level_other(3), 13, setbits[3])
-        stage(level_other(4), 14, setbits[4])
+        stage(level_other(1), 19, setbits[1])
+        stage(level_other(2), 21, setbits[2])
+        stage(level_other(3), 18, setbits[3])
+        stage(level_other(4), 16, setbits[4])
         stage(level_other(5), f7_lag - hop(1) + 2, setbits[5])
         return carry
 
@@ -694,8 +694,8 @@
     def dot01(a, m):
         return lax.dot_general(a, m, NN, precision=lax.Precision.HIGHEST, preferred_element_type=F32)
 
-    flux[0] = dot01(da, ones)
-    flux[1] = dot01(flow_sc[...], ones)
+    flux[0] = da
+    flux[1] = flow_sc[...]
     for i in range(1, 8):
         rflux(i).start()
 
@@ -705,11 +705,12 @@
         return carry
 
     lax.fori_loop(0, H, put, 0)
-    after = dot01(da, (s_i >= t_i).astype(F32)) + flux[1]
+    inside = dot01(da, (s_i >= t_i).astype(F32))
+    after = flux[1]
     for i in range(1, 8):
         rflux(i).wait_recv()
         after = after + rowf[i, 1] + jnp.where(row_from[i] > r, rowf[i, 0], 0.0)
-    ddecay_ref[...] = after
+    ddecay_ref[...] = inside + dot01(after, ones)
 
     def all_of(src, dst, send, recv):
         return copy(src, dst, send, recv, part)

time: 80 us -> 79.6 us (level)
  no operation moved by 1% of the time
where the time goes in v7:
time: 79.6 us; the launch traced here: 79.2 us
  Pallas kernels  78.6 us (99%)
    pallas_call x1, Pallas kernels, fused(): pl.pallas_call(fused_kernel, in_specs=[pl.BlockSpec(memory_space=pltpu.Me...  77.2 us

profile of v7, /device:TPU:1, one launch (start us, length us, event | category | flops | bytes accessed | tf_op | source)
XLA Modules:
  0.0 79.2 jit_solution(4920901103146396948)
XLA Ops:
  0.6 77.2 %fused.1 = (bf16[128,2048]{1,0:T(8,128)(2,1)S(1)}, bf16[128,2048]{1,0:T(8,128)(2,1)S(1)}, bf16[128,2048]{1,0:T(8,128)(2,1)S(1)}, bf16[128,2048]{1,0:T(8,128)(2,1...) custom-call(bf16[128,2048]{1,0:T(8,128)(2,1)} %q_in.1, bf16[128,2048]{1,0:T(8,128)(2,1)} %k_in.1, ...), custom_call_target="tpu_custom_call" | custom-call | tf_op jit(solution)/shard_map/fused/pallas_call | solution.py:763
  77.8 1.4 %finish.1 = (bf16[128,2048]{1,0:T(8,128)(2,1)}, bf16[128,2048]{1,0:T(8,128)(2,1)}, bf16[128,2048]{1,0:T(8,128)(2,1)}, bf16[128,2048]{1,0:T(8,128)(2,1)}, f32[14,16,128]{2,1,0:T(8,128)}, /*index=5*/f32[16,128]{1,0:T(8,128)}) custom-call(bf16[128,2048]{1,0:T(8,128)(2,1)S(1)} %get-tuple-element.12.refs_0_, bf16[128,2048]{1,0:T(8,128)(2,1)S(1)} %get-tuple-element.13.refs_1_, ...), custom_call_target="tpu_custom_call" | custom-call | tf_op jit(solution)/shard_map/finish/pallas_call | solution.py:795
